TPU v7x, 256 devices: a whole 4x4x8 slice. The times are simulated.
256 devices in a mesh: blk: 256 (over x, z, y, core).
Axes of the slice: x: 4, y: 4, z: 8, core: 2. Of those that a mesh axis runs over, the one named last changes fastest.
Arguments:
- diag_block: float32 [256, 512, 512], P('blk'), may hold values from -0.6 to 12.6, as said below
- near_blocks: float32 [256, 6, 512, 512], P('blk'), may hold values from -0.15 to 0.15
- far_coupling: float32 [256, 5, 256, 256], P('blk'), may hold values from -0.15 to 0.15
- leaf_basis: float32 [256, 512, 512], P('blk'), may hold values from -0.2 to 1.2
- parent_basis: float32 [65536, 1024], P('blk'), may hold values from -0.2 to 1.2
- near_index: int32 [256, 6], P('blk'), may hold values from 0 to 255, as said below
- far_index: int32 [256, 5], P('blk'), may hold values from 0 to 255, as said below
Outputs:
- leaf_factor: float32 [65536, 512], P('blk')
- parent_cholesky_factor: float32 [65536, 768], P('blk')
- parent_coupling: float32 [65536, 768], P('blk')
Inputs may be any that keep to these rules, and one draw needn't show every extreme that they name: `near_index`: row i lists 6 different leaves, none equal to i, among the 12 leaves of parents i // 4 - 1, i // 4, i // 4 + 1 (modulo 64). `far_index`: row i lists the remaining 5 leaves of those parents: i, its near list and its far list name each of the 12 leaves once. `diag_block`: each block is symmetric.
All inputs are finite; a program needn't handle non-finite values.
Results may differ from a plain program's by a relative error of at most 0.0003.
Values sent between devices are 32-bit elements; how exact they have to be, the bound alone decides.
A program may use at most 192 MiB of HBM per device.

v0:
```python
import jax
import jax.numpy as jnp
from jax import lax
from jax.sharding import PartitionSpec as P

LEAF = 512
RANK = 256
NEAR = 6
GROUP = 4
REDUN = 256
PAR = 1024
PRED = 768
FAR = 5


precise_mode = lax.Precision.HIGHEST


def passed_along(value, axis, steps):
    count = lax.axis_size(axis)
    pairs = [(source, (source + steps) % count) for source in range(count)]
    return lax.ppermute(value, axis, pairs)


def matmul(left_side, right_side):
    return jnp.dot(left_side, right_side, precision=precise_mode)


def factor_inverse(square):
    order = square.shape[0]
    if order <= 64:
        lower = jnp.linalg.cholesky(square)
        eye_block = jnp.eye(order, dtype=jnp.float32)
        inverse = lax.linalg.triangular_solve(lower, eye_block, left_side=True, lower=True)
        return (lower, inverse)
    half = order // 2
    upper_low, upper_inv = factor_inverse(square[:half, :half])
    below = matmul(square[half:, :half], upper_inv.T)
    rest = square[half:, half:] - matmul(below, below.T)
    rest = 0.5 * (rest + rest.T)
    rest_low, rest_inv = factor_inverse(rest)
    zero_block = jnp.zeros((half, order - half), jnp.float32)
    lower = jnp.concatenate(
        [
            jnp.concatenate([upper_low, zero_block], axis=1),
            jnp.concatenate([below, rest_low], axis=1),
        ],
        axis=0,
    )
    corner = -matmul(rest_inv, matmul(below, upper_inv))
    inverse = jnp.concatenate(
        [
            jnp.concatenate([upper_inv, zero_block], axis=1),
            jnp.concatenate([corner, rest_inv], axis=1),
        ],
        axis=0,
    )
    return (lower, inverse)


def sym_factor(square):
    return factor_inverse(0.5 * (square + square.T))


def select_block(stacked_blocks, position):
    return lax.dynamic_index_in_dim(stacked_blocks, position, 0, keepdims=False)


def split_close(vector):
    return (vector[: LEAF * RANK].reshape(LEAF, RANK), vector[LEAF * RANK :].reshape(RANK, PAR))


def split_far(vector):
    return (vector[: LEAF * RANK].reshape(LEAF, RANK), vector[LEAF * RANK :].reshape(RANK, RANK))


def on_device(
    diag_block, near_blocks, far_coupling, leaf_basis, parent_basis, near_index, far_index
):
    blocks = lax.axis_size("blk")
    myself = lax.axis_index("blk")
    member = myself % GROUP
    max_offset = 2 * GROUP - 1
    own_basis = leaf_basis[0]
    skeleton = own_basis[:, REDUN:]
    close_load = jnp.concatenate([skeleton.reshape(-1), parent_basis.reshape(-1)])
    far_load = jnp.concatenate([skeleton.reshape(-1), parent_basis[:, PRED:].reshape(-1)])
    received = {0: close_load}
    for offset in range(-max_offset, max_offset + 1):
        if 0 < abs(offset) < GROUP:
            received[offset] = passed_along(close_load, "blk", -offset)
        elif abs(offset) >= GROUP:
            received[offset] = passed_along(far_load, "blk", -offset)
    skel_list = []
    qskel_list = []
    qfull_list = []
    for offset in range(-max_offset, max_offset + 1):
        if abs(offset) < GROUP:
            skel_part, row_block = split_close(received[offset])
            qfull_list.append(row_block)
            qskel_list.append(row_block[:, PRED:])
        else:
            skel_part, row_block = split_far(received[offset])
            qskel_list.append(row_block)
        skel_list.append(skel_part)
    skel_stack = jnp.stack(skel_list)
    qskel_stack = jnp.stack(qskel_list)
    complete_basis_stack = jnp.stack(qfull_list)
    transformed = matmul(matmul(own_basis.T, diag_block[0]), own_basis)
    leaf_low, leaf_inv = sym_factor(transformed[:REDUN, :REDUN])
    coupled = matmul(leaf_inv, transformed[:REDUN, REDUN:])
    leaf_schur = transformed[REDUN:, REDUN:] - matmul(coupled.T, coupled)
    leaf_out = jnp.concatenate([leaf_low, coupled], axis=1)
    half_count = blocks // 2
    near_offset = (near_index[0] - myself + half_count) % blocks - half_count
    far_offset = (far_index[0] - myself + half_count) % blocks - half_count
    near_skel = jnp.take(skel_stack, near_offset + max_offset, axis=0)
    left_side_product = jnp.einsum("ar,mac->mrc", skeleton, near_blocks[0], precision=precise_mode)
    near_summands = jnp.einsum("mrc,mcs->mrs", left_side_product, near_skel, precision=precise_mode)
    columns = jnp.arange(3 * GROUP, dtype=jnp.int32)
    near_slots = jnp.arange(NEAR, dtype=jnp.int32)
    far_slots = NEAR + jnp.arange(FAR, dtype=jnp.int32)
    near_match = ((near_offset + GROUP + member)[:, None] == columns).astype(jnp.int32)
    far_match = ((far_offset + GROUP + member)[:, None] == columns).astype(jnp.int32)
    self_match = (columns == GROUP + member).astype(jnp.int32)
    source = (
        jnp.sum(near_match * near_slots[:, None], axis=0)
        + jnp.sum(far_match * far_slots[:, None], axis=0)
        + self_match * (NEAR + FAR)
    )
    all_blocks = jnp.concatenate([near_summands, far_coupling[0], leaf_schur[None]], axis=0)
    window_blocks = jnp.take(all_blocks, source, axis=0)
    children = jnp.arange(GROUP, dtype=jnp.int32)
    prev_rows = jnp.take(qskel_stack, children - GROUP - member + max_offset, axis=0)
    own_rows = jnp.take(complete_basis_stack, children - member + GROUP - 1, axis=0)
    next_rows = jnp.take(qskel_stack, children + GROUP - member + max_offset, axis=0)
    v_self = jnp.einsum(
        "bij,bjl->il", window_blocks[GROUP : 2 * GROUP], own_rows, precision=precise_mode
    )
    v_prev = jnp.einsum("bij,bjl->il", window_blocks[:GROUP], prev_rows, precision=precise_mode)
    v_next = jnp.einsum(
        "bij,bjl->il", window_blocks[2 * GROUP :], next_rows, precision=precise_mode
    )
    joined = jnp.concatenate([v_self, v_prev, v_next], axis=1)
    row_width = joined.shape[1]
    summand = matmul(parent_basis.T, joined)
    pieces = summand.reshape(GROUP, RANK, row_width)
    row_total = select_block(pieces, member)
    distances = list(range(1, GROUP)) + list(range(1 - GROUP, 0))
    for distance in distances:
        row_piece = select_block(pieces, (member + distance) % GROUP)
        arrived = passed_along(row_piece, "blk", distance)
        usable = (member - distance >= 0) & (member - distance < GROUP)
        row_total = row_total + jnp.where(usable, arrived, 0.0)
    own_part = row_total[:, :PAR]
    gathered = {0: own_part}
    for distance in distances:
        gathered[distance] = passed_along(own_part, "blk", distance)
    stacked_blocks = jnp.stack([gathered[distance] for distance in range(1 - GROUP, GROUP)])
    parent_block = jnp.take(stacked_blocks, member - children + GROUP - 1, axis=0).reshape(PAR, PAR)
    parent_low, parent_inv = sym_factor(parent_block[:PRED, :PRED])
    parent_coupled = matmul(parent_inv, parent_block[:PRED, PRED:])
    parent_trans = matmul(parent_inv, parent_block[PRED:, :PRED].T)
    parent_schur = parent_block[PRED:, PRED:] - matmul(parent_trans.T, parent_coupled)
    factor_all = jnp.concatenate([parent_low, parent_coupled.T], axis=0)
    factor_rows = lax.dynamic_slice_in_dim(factor_all, member * RANK, RANK, 0)
    edge_rows = jnp.where(member == GROUP - 1, parent_schur, row_total[:, PRED:PAR])
    coupling_rows = jnp.concatenate(
        [row_total[:, PAR : PAR + RANK], edge_rows, row_total[:, PAR + RANK :]], axis=1
    )
    return (leaf_out, factor_rows, coupling_rows)


def solution(mesh):
    placed = (
        P("blk", None, None),
        P("blk", None, None, None),
        P("blk", None, None, None),
        P("blk", None, None),
        P("blk", None),
        P("blk", None),
        P("blk", None),
    )
    return jax.shard_map(
        on_device,
        mesh=mesh,
        in_specs=placed,
        out_specs=(P("blk", None), P("blk", None), P("blk", None)),
        check_vma=False,
    )
```

profile of v0, /device:TPU:1, one launch (start us, length us, event | category | flops | bytes accessed | tf_op | source)
XLA Modules:
  0.0 933.4 jit_solution(10576734602882362954)
XLA Ops:
  23.6 5.9 cholesky.326
  31.4 4.9 custom-call.28
  39.9 6.6 cholesky.337
  48.4 5.5 custom-call.29
  60.4 5.9 cholesky.348
  68.2 4.9 custom-call.30
  74.2 5.8 cholesky.359
  82.4 4.9 custom-call.31
  93.0 5.6 collective-permute-start.10
  104.0 54.0 %collective-permute-done.10 = f32[196608]{0:T(1024)S(1)} collective-permute-done((f32[196608]{0:T(1024)}, f32[196608]{0:T(1024)S(1)}, u32[]{:S(2)}, u32[]{:S(2)}) %collective-permute-start.10) | collective-permute-done | bytes 786464 | tf_op jit(solution)/shard_map/ppermute | solution.py:22
  158.2 69.7 %collective-permute-start.7 = (f32[393216]{0:T(1024)}, f32[393216]{0:T(1024)}, u32[]{:S(2)}, u32[]{:S(2)}) collective-permute-start(f32[393216]{0:T(1024)} %constant_dynamic-update-slice_fusion.31), channel_id=1, source_target_pairs={{0,255},{1,0},{2,1},{3,2},{4,3},{5,4},{6,5},{7,6},{8,7},{9,8},{10,... | collective-permute-start | bytes 4718600 | tf_op jit(solution)/shard_map/ppermute | solution.py:22
  230.0 9.1 fusion
  367.4 3.8 gather_fusion.4
  378.1 5.8 gather_fusion
  383.8 5.2 fusion.5
  400.2 6.0 gather_fusion.2
  406.1 6.0 fusion.39
  414.5 5.2 fusion.20
  435.4 4.4 collective-permute-start.16
  442.8 8.1 collective-permute-start.17
  457.1 33.4 %collective-permute-start.19 = (f32[256,1536]{0,1:T(8,128)}, f32[256,1536]{0,1:T(8,128)}, u32[]{:S(2)}, u32[]{:S(2)}) collective-permute-start(f32[256,1536]{0,1:T(8,128)} %bitcast.504), channel_id=1, source_target_pairs={{0,255},{1,0},{2,1},{3,2},{4,3},{5,4},{6,5},{7,6},{8,7},{9,8},{10,... | collective-permute-start | bytes 4718600 | tf_op jit(solution)/shard_map/ppermute | solution.py:22
  492.1 34.1 %collective-permute-done.15 = f32[256,1536]{0,1:T(8,128)} collective-permute-done((f32[256,1536]{0,1:T(8,128)}, f32[256,1536]{0,1:T(8,128)}, u32[]{:S(2)}, u32[]{:S(2)}) %collective-permute-start.15) | collective-permute-done | bytes 1572896 | tf_op jit(solution)/shard_map/ppermute | solution.py:22
  526.2 7.1 collective-permute-done.16
  533.3 10.6 %collective-permute-done.17 = f32[256,1536]{0,1:T(8,128)} collective-permute-done((f32[256,1536]{0,1:T(8,128)}, f32[256,1536]{0,1:T(8,128)}, u32[]{:S(2)}, u32[]{:S(2)}) %collective-permute-start.17) | collective-permute-done | bytes 1572896 | tf_op jit(solution)/shard_map/ppermute | solution.py:22
  543.9 27.0 %collective-permute-done.18 = f32[256,1536]{0,1:T(8,128)} collective-permute-done((f32[256,1536]{0,1:T(8,128)}, f32[256,1536]{0,1:T(8,128)}, u32[]{:S(2)}, u32[]{:S(2)}) %collective-permute-start.18) | collective-permute-done | bytes 1572896 | tf_op jit(solution)/shard_map/ppermute | solution.py:22
  576.9 20.0 %collective-permute-start.22 = (f32[256,1024]{0,1:T(8,128)}, f32[256,1024]{0,1:T(8,128)S(1)}, u32[]{:S(2)}, u32[]{:S(2)}) collective-permute-start(f32[256,1024]{0,1:T(8,128)} %slice.707), channel_id=1, source_target_pairs={{0,255},{1,0},{2,1},{3,2},{4,3},{5,4},{6,5},{7,6},{8,7},{9,8},{10,... | collective-permute-start | bytes 3145736 | tf_op jit(solution)/shard_map/ppermute | solution.py:22
  602.1 11.6 %collective-permute-done.21 = f32[256,1024]{0,1:T(8,128)S(1)} collective-permute-done((f32[256,1024]{0,1:T(8,128)}, f32[256,1024]{0,1:T(8,128)S(1)}, u32[]{:S(2)}, u32[]{:S(2)}) %collective-permute-start.21) | collective-permute-done | bytes 1048608 | tf_op jit(solution)/shard_map/ppermute | solution.py:22
  616.8 4.3 collective-permute-done.23
  622.2 39.4 %collective-permute-done.24 = f32[256,1024]{0,1:T(8,128)S(1)} collective-permute-done((f32[256,1024]{0,1:T(8,128)}, f32[256,1024]{0,1:T(8,128)S(1)}, u32[]{:S(2)}, u32[]{:S(2)}) %collective-permute-start.24) | collective-permute-done | bytes 1048608 | tf_op jit(solution)/shard_map/ppermute | solution.py:22
  664.7 5.9 gather_fusion.5
  687.3 4.4 cholesky.370
  700.2 4.4 cholesky.381
  713.8 4.4 cholesky.392
  725.3 4.4 cholesky.403
  739.6 4.4 cholesky.414
  750.6 4.4 cholesky.425
  762.5 4.4 cholesky.436
  773.8 4.4 cholesky.447
  795.7 4.4 cholesky.458
  808.4 4.4 cholesky.469
  824.5 4.4 cholesky.480
  840.2 5.1 cholesky.491
  847.3 4.4 custom-call.43
  857.4 4.4 cholesky.502
  868.9 4.4 cholesky.513
  880.8 4.4 cholesky.524
  891.9 4.4 cholesky.535
  906.2 8.3 fusion.63
  (701 shorter events, 425.4 us)
Async XLA Ops:
  0.6 17.2 %copy-start = (f32[1,512,512]{2,1,0:T(8,128)S(1)}, f32[1,512,512]{2,1,0:T(8,128)}, u32[]{:S(2)}) copy-start(f32[1,512,512]{2,1,0:T(8,128)} %param.17) | copy-start | bytes 3145732
  3.2 14.6 %copy-start.2 = (f32[1,512,512]{2,1,0:T(8,128)S(1)}, f32[1,512,512]{2,1,0:T(8,128)}, u32[]{:S(2)}) copy-start(f32[1,512,512]{2,1,0:T(8,128)} %param.20) | copy-start | bytes 3145732
  4.1 88.9 %collective-permute-start = (f32[196608]{0:T(1024)}, f32[196608]{0:T(1024)}, u32[]{:S(2)}, u32[]{:S(2)}) collective-permute-start(f32[196608]{0:T(1024)} %constant_dynamic-update-slice_fusion.30), channel_id=1, source_target_pairs={{0,7},{1,8},{2,9},{3,10},{4,11},{5,12},{6,13},{7,14},{8,15},{9,16}... | collective-permute-start | bytes 2359304 | tf_op jit(solution)/shard_map/ppermute | solution.py:22
  7.1 91.4 %collective-permute-start.1 = (f32[196608]{0:T(1024)}, f32[196608]{0:T(1024)}, u32[]{:S(2)}, u32[]{:S(2)}) collective-permute-start(f32[196608]{0:T(1024)} %constant_dynamic-update-slice_fusion.30), channel_id=1, source_target_pairs={{0,6},{1,7},{2,8},{3,9},{4,10},{5,11},{6,12},{7,13},{8,14},{9,15},... | collective-permute-start | bytes 2359304 | tf_op jit(solution)/shard_map/ppermute | solution.py:22
  9.8 88.7 %collective-permute-start.2 = (f32[196608]{0:T(1024)}, f32[196608]{0:T(1024)}, u32[]{:S(2)}, u32[]{:S(2)}) collective-permute-start(f32[196608]{0:T(1024)} %constant_dynamic-update-slice_fusion.30), channel_id=1, source_target_pairs={{0,5},{1,6},{2,7},{3,8},{4,9},{5,10},{6,11},{7,12},{8,13},{9,14},{... | collective-permute-start | bytes 2359304 | tf_op jit(solution)/shard_map/ppermute | solution.py:22
  11.6 87.9 %collective-permute-start.3 = (f32[196608]{0:T(1024)}, f32[196608]{0:T(1024)}, u32[]{:S(2)}, u32[]{:S(2)}) collective-permute-start(f32[196608]{0:T(1024)} %constant_dynamic-update-slice_fusion.30), channel_id=1, source_target_pairs={{0,4},{1,5},{2,6},{3,7},{4,8},{5,9},{6,10},{7,11},{8,12},{9,13},{1... | collective-permute-start | bytes 2359304 | tf_op jit(solution)/shard_map/ppermute | solution.py:22
  15.4 213.4 %collective-permute-start.4 = (f32[393216]{0:T(1024)}, f32[393216]{0:T(1024)}, u32[]{:S(2)}, u32[]{:S(2)}) collective-permute-start(f32[393216]{0:T(1024)} %constant_dynamic-update-slice_fusion.31), channel_id=1, source_target_pairs={{0,3},{1,4},{2,5},{3,6},{4,7},{5,8},{6,9},{7,10},{8,11},{9,12},{10... | collective-permute-start | bytes 4718600 | tf_op jit(solution)/shard_map/ppermute | solution.py:22
  21.5 66.1 %copy-start.90 = (s32[1,6]{1,0:T(1,128)S(1)}, s32[1,6]{1,0:T(1,128)}, u32[]{:S(2)}) copy-start(s32[1,6]{1,0:T(1,128)} %param.22) | copy-start | bytes 76
  21.6 66.1 %copy-start.91 = (s32[1,5]{1,0:T(1,128)S(1)}, s32[1,5]{1,0:T(1,128)}, u32[]{:S(2)}) copy-start(s32[1,5]{1,0:T(1,128)} %param.23) | copy-start | bytes 64
  88.0 15.4 %copy-start.87 = (s32[12]{0:T(128)}, s32[12]{0:T(128)S(1)}, u32[]{:S(2)}) copy-start(s32[12]{0:T(128)S(1)} %select_reduce_fusion.20) | copy-start | bytes 148
  93.0 65.1 %collective-permute-start.10 = (f32[196608]{0:T(1024)}, f32[196608]{0:T(1024)S(1)}, u32[]{:S(2)}, u32[]{:S(2)}) collective-permute-start(f32[196608]{0:T(1024)} %constant_dynamic-update-slice_fusion.30), channel_id=1, source_target_pairs={{0,252},{1,253},{2,254},{3,255},{4,0},{5,1},{6,2},{7,3},{8,4},{9,5... | collective-permute-start | bytes 2359304 | tf_op jit(solution)/shard_map/ppermute | solution.py:22
  98.5 59.5 %collective-permute-start.11 = (f32[196608]{0:T(1024)}, f32[196608]{0:T(1024)}, u32[]{:S(2)}, u32[]{:S(2)}) collective-permute-start(f32[196608]{0:T(1024)} %constant_dynamic-update-slice_fusion.30), channel_id=1, source_target_pairs={{0,251},{1,252},{2,253},{3,254},{4,255},{5,0},{6,1},{7,2},{8,3},{9... | collective-permute-start | bytes 2359304 | tf_op jit(solution)/shard_map/ppermute | solution.py:22
  98.5 59.6 %collective-permute-start.12 = (f32[196608]{0:T(1024)}, f32[196608]{0:T(1024)}, u32[]{:S(2)}, u32[]{:S(2)}) collective-permute-start(f32[196608]{0:T(1024)} %constant_dynamic-update-slice_fusion.30), channel_id=1, source_target_pairs={{0,250},{1,251},{2,252},{3,253},{4,254},{5,255},{6,0},{7,1},{8,2},... | collective-permute-start | bytes 2359304 | tf_op jit(solution)/shard_map/ppermute | solution.py:22
  99.4 128.5 %collective-permute-start.13 = (f32[196608]{0:T(1024)}, f32[196608]{0:T(1024)}, u32[]{:S(2)}, u32[]{:S(2)}) collective-permute-start(f32[196608]{0:T(1024)} %constant_dynamic-update-slice_fusion.30), channel_id=1, source_target_pairs={{0,249},{1,250},{2,251},{3,252},{4,253},{5,254},{6,255},{7,0},{8,1... | collective-permute-start | bytes 2359304 | tf_op jit(solution)/shard_map/ppermute | solution.py:22
  158.1 71.9 %copy-start.39 = (f32[196608]{0:T(1024)}, f32[196608]{0:T(1024)S(1)}, u32[]{:S(2)}) copy-start(f32[196608]{0:T(1024)S(1)} %collective-permute-done.10) | copy-start | bytes 2359300
  158.1 149.4 %collective-permute-start.5 = (f32[393216]{0:T(1024)}, f32[393216]{0:T(1024)}, u32[]{:S(2)}, u32[]{:S(2)}) collective-permute-start(f32[393216]{0:T(1024)} %constant_dynamic-update-slice_fusion.31), channel_id=1, source_target_pairs={{0,2},{1,3},{2,4},{3,5},{4,6},{5,7},{6,8},{7,9},{8,10},{9,11},{10,... | collective-permute-start | bytes 4718600 | tf_op jit(solution)/shard_map/ppermute | solution.py:22
  158.1 153.0 %collective-permute-start.6 = (f32[393216]{0:T(1024)}, f32[393216]{0:T(1024)}, u32[]{:S(2)}, u32[]{:S(2)}) collective-permute-start(f32[393216]{0:T(1024)} %constant_dynamic-update-slice_fusion.31), channel_id=1, source_target_pairs={{0,1},{1,2},{2,3},{3,4},{4,5},{5,6},{6,7},{7,8},{8,9},{9,10},{10,1... | collective-permute-start | bytes 4718600 | tf_op jit(solution)/shard_map/ppermute | solution.py:22
  158.2 156.5 %collective-permute-start.7 = (f32[393216]{0:T(1024)}, f32[393216]{0:T(1024)}, u32[]{:S(2)}, u32[]{:S(2)}) collective-permute-start(f32[393216]{0:T(1024)} %constant_dynamic-update-slice_fusion.31), channel_id=1, source_target_pairs={{0,255},{1,0},{2,1},{3,2},{4,3},{5,4},{6,5},{7,6},{8,7},{9,8},{10,... | collective-permute-start | bytes 4718600 | tf_op jit(solution)/shard_map/ppermute | solution.py:22
  227.9 90.4 %collective-permute-start.8 = (f32[393216]{0:T(1024)}, f32[393216]{0:T(1024)}, u32[]{:S(2)}, u32[]{:S(2)}) collective-permute-start(f32[393216]{0:T(1024)} %constant_dynamic-update-slice_fusion.31), channel_id=1, source_target_pairs={{0,254},{1,255},{2,0},{3,1},{4,2},{5,3},{6,4},{7,5},{8,6},{9,7},{1... | collective-permute-start | bytes 4718600 | tf_op jit(solution)/shard_map/ppermute | solution.py:22
  228.8 93.2 %collective-permute-start.9 = (f32[393216]{0:T(1024)}, f32[393216]{0:T(1024)}, u32[]{:S(2)}, u32[]{:S(2)}) collective-permute-start(f32[393216]{0:T(1024)} %constant_dynamic-update-slice_fusion.31), channel_id=1, source_target_pairs={{0,253},{1,254},{2,255},{3,0},{4,1},{5,2},{6,3},{7,4},{8,5},{9,6},... | collective-permute-start | bytes 4718600 | tf_op jit(solution)/shard_map/ppermute | solution.py:22
  349.3 12.2 %copy-start.35 = (f32[1,256,256]{2,1,0:T(8,128)S(1)}, f32[1,256,256]{2,1,0:T(8,128)}, u32[]{:S(2)}) copy-start(f32[1,256,256]{2,1,0:T(8,128)} %slice.597) | copy-start | bytes 786436
  349.3 12.9 %copy-start.36 = (f32[1,256,256]{2,1,0:T(8,128)S(1)}, f32[1,256,256]{2,1,0:T(8,128)}, u32[]{:S(2)}) copy-start(f32[1,256,256]{2,1,0:T(8,128)} %slice.599) | copy-start | bytes 786436
  349.4 13.5 %copy-start.37 = (f32[1,256,256]{2,1,0:T(8,128)S(1)}, f32[1,256,256]{2,1,0:T(8,128)}, u32[]{:S(2)}) copy-start(f32[1,256,256]{2,1,0:T(8,128)} %slice.601) | copy-start | bytes 786436
  426.2 30.9 %collective-permute-start.14 = (f32[256,1536]{0,1:T(8,128)}, f32[256,1536]{0,1:T(8,128)}, u32[]{:S(2)}, u32[]{:S(2)}) collective-permute-start(f32[256,1536]{0,1:T(8,128)} %bitcast.505), channel_id=1, source_target_pairs={{0,1},{1,2},{2,3},{3,4},{4,5},{5,6},{6,7},{7,8},{8,9},{9,10},{10,1... | collective-permute-start | bytes 4718600 | tf_op jit(solution)/shard_map/ppermute | solution.py:22
  430.3 95.9 %collective-permute-start.15 = (f32[256,1536]{0,1:T(8,128)}, f32[256,1536]{0,1:T(8,128)}, u32[]{:S(2)}, u32[]{:S(2)}) collective-permute-start(f32[256,1536]{0,1:T(8,128)} %bitcast.500), channel_id=1, source_target_pairs={{0,2},{1,3},{2,4},{3,5},{4,6},{5,7},{6,8},{7,9},{8,10},{9,11},{10,... | collective-permute-start | bytes 4718600 | tf_op jit(solution)/shard_map/ppermute | solution.py:22
  435.4 97.9 %collective-permute-start.16 = (f32[256,1536]{0,1:T(8,128)}, f32[256,1536]{0,1:T(8,128)}, u32[]{:S(2)}, u32[]{:S(2)}) collective-permute-start(f32[256,1536]{0,1:T(8,128)} %bitcast.501), channel_id=1, source_target_pairs={{0,3},{1,4},{2,5},{3,6},{4,7},{5,8},{6,9},{7,10},{8,11},{9,12},{10... | collective-permute-start | bytes 4718600 | tf_op jit(solution)/shard_map/ppermute | solution.py:22
  442.8 101.1 %collective-permute-start.17 = (f32[256,1536]{0,1:T(8,128)}, f32[256,1536]{0,1:T(8,128)}, u32[]{:S(2)}, u32[]{:S(2)}) collective-permute-start(f32[256,1536]{0,1:T(8,128)} %bitcast.502), channel_id=1, source_target_pairs={{0,253},{1,254},{2,255},{3,0},{4,1},{5,2},{6,3},{7,4},{8,5},{9,6},... | collective-permute-start | bytes 4718600 | tf_op jit(solution)/shard_map/ppermute | solution.py:22
  454.0 116.9 %collective-permute-start.18 = (f32[256,1536]{0,1:T(8,128)}, f32[256,1536]{0,1:T(8,128)}, u32[]{:S(2)}, u32[]{:S(2)}) collective-permute-start(f32[256,1536]{0,1:T(8,128)} %bitcast.503), channel_id=1, source_target_pairs={{0,254},{1,255},{2,0},{3,1},{4,2},{5,3},{6,4},{7,5},{8,6},{9,7},{1... | collective-permute-start | bytes 4718600 | tf_op jit(solution)/shard_map/ppermute | solution.py:22
  457.1 113.8 %collective-permute-start.19 = (f32[256,1536]{0,1:T(8,128)}, f32[256,1536]{0,1:T(8,128)}, u32[]{:S(2)}, u32[]{:S(2)}) collective-permute-start(f32[256,1536]{0,1:T(8,128)} %bitcast.504), channel_id=1, source_target_pairs={{0,255},{1,0},{2,1},{3,2},{4,3},{5,4},{6,5},{7,6},{8,7},{9,8},{10,... | collective-permute-start | bytes 4718600 | tf_op jit(solution)/shard_map/ppermute | solution.py:22
  492.1 83.7 %copy-start.66 = (f32[64,64]{1,0:T(8,128)S(1)}, f32[64,64]{1,0:T(8,128)}, u32[]{:S(2)}) copy-start(f32[64,64]{1,0:T(8,128)} %get-tuple-element.56) | copy-start | bytes 49156
  492.1 83.7 %copy-start.67 = (f32[64,64]{1,0:T(8,128)S(1)}, f32[64,64]{1,0:T(8,128)}, u32[]{:S(2)}) copy-start(f32[64,64]{1,0:T(8,128)} %get-tuple-element.54) | copy-start | bytes 49156
  492.1 83.8 %copy-start.68 = (f32[64,64]{1,0:T(8,128)S(1)}, f32[64,64]{1,0:T(8,128)}, u32[]{:S(2)}) copy-start(f32[64,64]{1,0:T(8,128)} %get-tuple-element.52) | copy-start | bytes 49156
  492.1 83.8 %copy-start.69 = (f32[64,64]{1,0:T(8,128)S(1)}, f32[64,64]{1,0:T(8,128)}, u32[]{:S(2)}) copy-start(f32[64,64]{1,0:T(8,128)} %get-tuple-element.50) | copy-start | bytes 49156
  575.5 23.8 %collective-permute-start.20 = (f32[256,1024]{0,1:T(8,128)}, f32[256,1024]{0,1:T(8,128)}, u32[]{:S(2)}, u32[]{:S(2)}) collective-permute-start(f32[256,1024]{0,1:T(8,128)} %slice.707), channel_id=1, source_target_pairs={{0,253},{1,254},{2,255},{3,0},{4,1},{5,2},{6,3},{7,4},{8,5},{9,6},... | collective-permute-start | bytes 3145736 | tf_op jit(solution)/shard_map/ppermute | solution.py:22
  575.9 37.8 %collective-permute-start.21 = (f32[256,1024]{0,1:T(8,128)}, f32[256,1024]{0,1:T(8,128)S(1)}, u32[]{:S(2)}, u32[]{:S(2)}) collective-permute-start(f32[256,1024]{0,1:T(8,128)} %slice.707), channel_id=1, source_target_pairs={{0,254},{1,255},{2,0},{3,1},{4,2},{5,3},{6,4},{7,5},{8,6},{9,7},{1... | collective-permute-start | bytes 3145736 | tf_op jit(solution)/shard_map/ppermute | solution.py:22
  576.9 37.9 %collective-permute-start.22 = (f32[256,1024]{0,1:T(8,128)}, f32[256,1024]{0,1:T(8,128)S(1)}, u32[]{:S(2)}, u32[]{:S(2)}) collective-permute-start(f32[256,1024]{0,1:T(8,128)} %slice.707), channel_id=1, source_target_pairs={{0,255},{1,0},{2,1},{3,2},{4,3},{5,4},{6,5},{7,6},{8,7},{9,8},{10,... | collective-permute-start | bytes 3145736 | tf_op jit(solution)/shard_map/ppermute | solution.py:22
  598.5 22.6 %collective-permute-start.23 = (f32[256,1024]{0,1:T(8,128)}, f32[256,1024]{0,1:T(8,128)S(1)}, u32[]{:S(2)}, u32[]{:S(2)}) collective-permute-start(f32[256,1024]{0,1:T(8,128)} %slice.707), channel_id=1, source_target_pairs={{0,1},{1,2},{2,3},{3,4},{4,5},{5,6},{6,7},{7,8},{8,9},{9,10},{10,1... | collective-permute-start | bytes 3145736 | tf_op jit(solution)/shard_map/ppermute | solution.py:22
  598.5 63.0 %collective-permute-start.24 = (f32[256,1024]{0,1:T(8,128)}, f32[256,1024]{0,1:T(8,128)S(1)}, u32[]{:S(2)}, u32[]{:S(2)}) collective-permute-start(f32[256,1024]{0,1:T(8,128)} %slice.707), channel_id=1, source_target_pairs={{0,2},{1,3},{2,4},{3,5},{4,6},{5,7},{6,8},{7,9},{8,10},{9,11},{10,... | collective-permute-start | bytes 3145736 | tf_op jit(solution)/shard_map/ppermute | solution.py:22
  599.4 64.3 %collective-permute-start.25 = (f32[256,1024]{0,1:T(8,128)}, f32[256,1024]{0,1:T(8,128)S(1)}, u32[]{:S(2)}, u32[]{:S(2)}) collective-permute-start(f32[256,1024]{0,1:T(8,128)} %slice.707), channel_id=1, source_target_pairs={{0,3},{1,4},{2,5},{3,6},{4,7},{5,8},{6,9},{7,10},{8,11},{9,12},{10... | collective-permute-start | bytes 3145736 | tf_op jit(solution)/shard_map/ppermute | solution.py:22
  750.0 34.2 %copy-start.48 = (f32[48,48]{1,0:T(8,128)}, f32[48,48]{1,0:T(8,128)S(1)}, u32[]{:S(2)}) copy-start(f32[48,48]{1,0:T(8,128)S(1)} %fusion.255) | copy-start | bytes 27652
  794.8 60.0 %copy-start.27 = (f32[384,384]{0,1:T(8,128)S(1)}, f32[384,384]{0,1:T(8,128)}, u32[]{:S(2)}) copy-start(f32[384,384]{0,1:T(8,128)} %copy-done.26) | copy-start | bytes 1769476
  820.1 35.3 %copy-start.31 = (f32[96,96]{0,1:T(8,128)}, f32[96,96]{0,1:T(8,128)S(1)}, u32[]{:S(2)}) copy-start(f32[96,96]{0,1:T(8,128)S(1)} %fusion.202) | copy-start | bytes 110596
  835.0 20.5 %copy-start.44 = (f32[48,48]{1,0:T(8,128)}, f32[48,48]{1,0:T(8,128)S(1)}, u32[]{:S(2)}) copy-start(f32[48,48]{1,0:T(8,128)S(1)} %fusion.249) | copy-start | bytes 27652
  857.0 34.6 %copy-start.38 = (f32[192,192]{1,0:T(8,128)S(1)}, f32[192,192]{1,0:T(8,128)}, u32[]{:S(2)}) copy-start(f32[192,192]{1,0:T(8,128)} %select_maximum_fusion.7) | copy-start | bytes 442372
  891.2 14.9 %copy-start.40 = (f32[48,48]{1,0:T(8,128)}, f32[48,48]{1,0:T(8,128)S(1)}, u32[]{:S(2)}) copy-start(f32[48,48]{1,0:T(8,128)S(1)} %fusion.245) | copy-start | bytes 27652
  891.6 14.6 %copy-start.61 = (f32[48,96]{1,0:T(8,128)}, f32[48,96]{1,0:T(8,128)S(1)}, u32[]{:S(2)}) copy-start(f32[48,96]{1,0:T(8,128)S(1)} %concatenate.445) | copy-start | bytes 55300
  891.6 14.6 %copy-start.58 = (f32[96,192]{1,0:T(8,128)}, f32[96,192]{1,0:T(8,128)S(1)}, u32[]{:S(2)}) copy-start(f32[96,192]{1,0:T(8,128)S(1)} %concatenate.444) | copy-start | bytes 221188
  891.7 14.5 %copy-start.60 = (f32[192,384]{1,0:T(8,128)}, f32[192,384]{1,0:T(8,128)S(1)}, u32[]{:S(2)}) copy-start(f32[192,384]{1,0:T(8,128)S(1)} %concatenate.443) | copy-start | bytes 884740
  (72 other events, 253.3 us)
where the time goes:
time: 951 us; the launch traced here: 933 us
  other arithmetic  247 us (26%)
  local copies, waits for them, and re-layouts  236 us (25%)
  waiting for transfers between devices  189 us (20%)
  starting transfers between devices  164 us (17%)
  matrix products  94.6 us (10%)
    ppermute x26, waiting for transfers between devices, passed_along(): return lax.ppermute(value, axis, pairs)  189 us
    ppermute x26, starting transfers between devices, passed_along(): return lax.ppermute(value, axis, pairs)  164 us
    another operation x60, other arithmetic, factor_inverse(): lower = jnp.linalg.cholesky(square)  109 us
    another operation x40, other arithmetic, factor_inverse(): lax.linalg.triangular_solve(lower, eye_block, left_side=True, lower=True)  105 us
    unnamed x243, local copies, waits for them, and re-layouts  77.4 us
    dot_general x80, matrix products, matmul(): return jnp.dot(left_side, right_side, precision=precise_mode)  66.2 us
    slice x16, local copies, waits for them, and re-layouts, split_far(): vector[LEAF * RANK:].reshape(RANK, RANK)  27.1 us
  transfers between devices with their start and end apart: 26, of which 9 were waited for; matrix products, arithmetic and copies ran while one was open for 21% of the time, Pallas kernels for 0%

commit v1 on v0

v1 whole, which is shorter than its diff:
```python
import jax
import jax.numpy as jnp
from jax import lax
from jax.experimental import pallas as pl
from jax.experimental.pallas import tpu as pltpu
from jax.sharding import PartitionSpec as P

LEAF = 512
RANK = 256
NEAR = 6
GROUP = 4
REDUN = 256
PAR = 1024
PRED = 768
FAR = 5
TILE = 128
F32 = jnp.float32
BF16 = jnp.bfloat16
NN = (((1,), (0,)), ((), ()))
NT = (((1,), (1,)), ((), ()))
TN = (((0,), (0,)), ((), ()))


def split2(x):
    high = x.astype(BF16)
    return high, (x - high.astype(F32)).astype(BF16)


def dot_split(a, b, dims):
    (ah, al), (bh, bl) = a, b
    out = lax.dot_general(ah, bh, dims, preferred_element_type=F32)
    out += lax.dot_general(ah, bl, dims, preferred_element_type=F32)
    return out + lax.dot_general(al, bh, dims, preferred_element_type=F32)


def dot3(a, b, dims):
    return dot_split(split2(a), split2(b), dims)


def chol_tile(square):
    n, k = TILE, 32
    sub = lax.broadcasted_iota(jnp.int32, (k, n), 0)
    lane = lax.broadcasted_iota(jnp.int32, (k, n), 1)
    uppers, inverses = [], []
    rest, rest_inv = square, None
    for window in range(n // k):
        j0 = window * k
        rows = rest[:k]
        eye = (lane == sub + j0).astype(F32)
        inv = eye if rest_inv is None else rest_inv[:k] + eye
        cols = [jnp.broadcast_to(rows[:, j0 + c : j0 + c + 1], (k, n)) for c in range(k)]
        for c in range(k):
            base = c // 8 * 8
            height = k - base
            pivot = jnp.broadcast_to(cols[c][c - base : c - base + 1, :], (8, n))
            scale = lax.rsqrt(pivot)
            tall = jnp.concatenate([scale] * (height // 8), 0)
            low = jnp.where(sub[base:] > c, cols[c] * tall, 0.0)
            row_u = jnp.broadcast_to(rows[c - base : c - base + 1, :], (8, n)) * scale
            row_i = jnp.broadcast_to(inv[c - base : c - base + 1, :], (8, n)) * scale
            for e in range(c + 1, k):
                cols[e] = cols[e] - low * jnp.broadcast_to(low[e - base : e - base + 1, :], (height, n))
            row_u = jnp.concatenate([row_u] * (height // 8), 0)
            row_i = jnp.concatenate([row_i] * (height // 8), 0)
            rows = jnp.where(sub[base:] == c, row_u, rows - low * row_u)
            inv = jnp.where(sub[base:] == c, row_i, inv - low * row_i)
            if c % 8 == 7:
                uppers.append(rows[:8])
                inverses.append(inv[:8])
                rows, inv = rows[8:], inv[8:]
                cols = [col[8:] if col.shape[0] > 8 else col for col in cols]
        done = jnp.concatenate(uppers[-(k // 8) :], 0)
        done_inv = jnp.concatenate(inverses[-(k // 8) :], 0)
        done = jnp.where(lane >= sub + j0, done, 0.0)
        del uppers[-(k // 8) :]
        uppers.append(done)
        if j0 + k < n:
            both = jnp.concatenate([done, done_inv], axis=1)
            hi = both.astype(BF16)
            left = both - hi.astype(F32)
            mid = left.astype(BF16)
            lo = (left - mid.astype(F32)).astype(BF16)
            lhs = jnp.concatenate([hi[:, :n], hi[:, :n], mid[:, :n], hi[:, :n], lo[:, :n], mid[:, :n]], axis=0)
            rhs = jnp.concatenate([hi, mid, hi, lo, hi, mid], axis=0)
            update = lax.dot_general(lhs, rhs, TN, preferred_element_type=F32)[j0 + k :]
            rest = rest[k:] - update[:, :n]
            rest_inv = -update[:, n:] if rest_inv is None else rest_inv[k:] - update[:, n:]
    return jnp.concatenate(uppers, 0), jnp.concatenate(inverses, 0)


def leaf_kernel(diag_ref, basis_ref, out_ref, schur_ref):
    basis = split2(basis_ref[...])
    right = split2(dot_split(split2(diag_ref[...]), basis, NN))
    top = dot_split([q[:, :REDUN] for q in basis], right, TN)
    low_part = [q[:, REDUN:] for q in right]
    corner = dot_split([q[:, REDUN:] for q in basis], low_part, TN)
    upper, inverse = chol_tile(top[:TILE, :TILE])
    out_ref[:TILE, :TILE] = upper.T
    out_ref[:TILE, TILE:REDUN] = jnp.zeros((TILE, TILE), F32)
    across = dot3(inverse, top[:TILE, TILE:], NN)
    out_ref[TILE:, :TILE] = across[:, :TILE].T
    out_ref[:TILE, REDUN:] = across[:, TILE:]
    parts = split2(across)
    rest = top[TILE:, TILE:] - dot_split([q[:, :TILE] for q in parts], parts, TN)
    upper, inverse = chol_tile(rest[:, :TILE])
    out_ref[TILE:, TILE:REDUN] = upper.T
    across2 = dot3(inverse, rest[:, TILE:], NN)
    out_ref[TILE:, REDUN:] = across2
    coupled = split2(out_ref[:, REDUN:])
    schur_ref[...] = corner - dot_split(coupled, coupled, TN)


def window_kernel(index_ref, source_ref, basis_ref, near_ref, far_ref, schur_ref, skel_ref, rows_ref, prev_ref, next_ref, out_ref, blocks):
    skeleton = split2(basis_ref[:, REDUN:])

    def one_near(slot, carry):
        left = dot_split(skeleton, split2(near_ref[slot]), TN)
        blocks[slot] = dot3(left, skel_ref[index_ref[slot]], NN)
        return carry

    lax.fori_loop(0, NEAR, one_near, 0)
    for slot in range(FAR):
        blocks[NEAR + slot] = far_ref[slot]
    blocks[NEAR + FAR] = schur_ref[...]

    def term(column, rows):
        return dot3(blocks[source_ref[column]], rows, NN)

    for half in range(2):
        cols = slice(half * 512, half * 512 + 512)
        total = term(GROUP, rows_ref[0][:, cols])
        for child in range(1, GROUP):
            total += term(GROUP + child, rows_ref[child][:, cols])
        out_ref[:, cols] = total
    for base, ref, at in ((0, prev_ref, PAR), (2 * GROUP, next_ref, PAR + RANK)):
        total = term(base, ref[0])
        for child in range(1, GROUP):
            total += term(base + child, ref[child])
        out_ref[:, at : at + RANK] = total


def parent_kernel(member_ref, rows_ref, v_ref, factor_ref, couple_ref, basis_hi, basis_lo, v_hi, v_lo, c_ref, low_ref, low_hi, low_lo):
    member = member_ref[0]
    rows = PAR + RANK
    for child in range(GROUP):
        at = slice(child * RANK, child * RANK + RANK)
        basis_hi[at, :], basis_lo[at, :] = split2(rows_ref[child])
        v_hi[at, :], v_lo[at, :] = split2(v_ref[child])

    def piece(step, carry):
        at = pl.ds(pl.multiple_of(step * RANK, RANK), RANK)
        left = (basis_hi[:, at], basis_lo[:, at])
        c_ref[at, :] = dot_split(left, (v_hi[:, :PAR], v_lo[:, :PAR]), TN)
        return carry

    lax.fori_loop(0, GROUP, piece, 0)
    mine = pl.ds(pl.multiple_of(member * RANK, RANK), RANK)
    sides = dot_split((basis_hi[:, mine], basis_lo[:, mine]), (v_hi[:, PAR:], v_lo[:, PAR:]), TN)
    couple_ref[:, :RANK] = sides[:, :RANK]
    couple_ref[:, 2 * RANK :] = sides[:, RANK:]
    couple_ref[:, RANK : 2 * RANK] = c_ref[mine, PRED:]
    for j in range(PRED // TILE):
        cols = slice(j * TILE, j * TILE + TILE)
        for i in range(j, PRED // TILE):
            here = slice(i * TILE, i * TILE + TILE)
            low_ref[here, cols] = 0.5 * (c_ref[here, cols] + c_ref[cols, here].T)
            if i > j:
                low_ref[cols, here] = jnp.zeros((TILE, TILE), F32)
        for half in range(2):
            there = slice(PRED + half * TILE, PRED + half * TILE + TILE)
            low_ref[there, cols] = c_ref[cols, there].T
        low_ref[PAR:, cols] = c_ref[PRED:, cols]
    for b in range(PRED // TILE):
        cols = slice(b * TILE, b * TILE + TILE)
        strip = low_ref[b * TILE :, cols]
        if b:
            done = slice(0, b * TILE)
            left = (low_hi[b * TILE :, done], low_lo[b * TILE :, done])
            strip = strip - dot_split(left, (left[0][:TILE], left[1][:TILE]), NT)
        upper, inverse = chol_tile(strip[:TILE])
        low_ref[cols, cols] = upper.T
        below = dot3(strip[TILE:], inverse, NT)
        low_ref[(b + 1) * TILE :, cols] = below
        low_hi[(b + 1) * TILE :, cols], low_lo[(b + 1) * TILE :, cols] = split2(below)
    factor_ref[...] = low_ref[mine, :]

    @pl.when(member == GROUP - 1)
    def _():
        left = (low_hi[PAR:, :], low_lo[PAR:, :])
        right = (low_hi[PRED:PAR, :], low_lo[PRED:PAR, :])
        couple_ref[:, RANK : 2 * RANK] = c_ref[PRED:, PRED:] - dot_split(left, right, NT)


def passed_along(value, axis, steps):
    count = lax.axis_size(axis)
    pairs = [(source, (source + steps) % count) for source in range(count)]
    return lax.ppermute(value, axis, pairs)


def split_close(vector):
    return (vector[: LEAF * RANK].reshape(LEAF, RANK), vector[LEAF * RANK :].reshape(RANK, PAR))


def split_far(vector):
    return (vector[: LEAF * RANK].reshape(LEAF, RANK), vector[LEAF * RANK :].reshape(RANK, RANK))


def shape(*dims):
    return jax.ShapeDtypeStruct(dims, F32)


def vmem(count):
    return [pl.BlockSpec(memory_space=pltpu.VMEM)] * count


SMEM = pl.BlockSpec(memory_space=pltpu.SMEM)


def on_device(diag_block, near_blocks, far_coupling, leaf_basis, parent_basis, near_index, far_index):
    blocks = lax.axis_size("blk")
    myself = lax.axis_index("blk")
    member = myself % GROUP
    max_offset = 2 * GROUP - 1
    own_basis = leaf_basis[0]
    skeleton = own_basis[:, REDUN:]
    close_load = jnp.concatenate([skeleton.reshape(-1), parent_basis.reshape(-1)])
    far_load = jnp.concatenate([skeleton.reshape(-1), parent_basis[:, PRED:].reshape(-1)])
    received = {0: close_load}
    for offset in range(-max_offset, max_offset + 1):
        if 0 < abs(offset) < GROUP:
            received[offset] = passed_along(close_load, "blk", -offset)
        elif abs(offset) >= GROUP:
            received[offset] = passed_along(far_load, "blk", -offset)
    skel_list = []
    qskel_list = []
    qfull_list = []
    for offset in range(-max_offset, max_offset + 1):
        if abs(offset) < GROUP:
            skel_part, row_block = split_close(received[offset])
            qfull_list.append(row_block)
            qskel_list.append(row_block[:, PRED:])
        else:
            skel_part, row_block = split_far(received[offset])
            qskel_list.append(row_block)
        skel_list.append(skel_part)
    skel_stack = jnp.stack(skel_list)
    qskel_stack = jnp.stack(qskel_list)
    complete_basis_stack = jnp.stack(qfull_list)

    leaf_out, leaf_schur = pl.pallas_call(
        leaf_kernel,
        out_shape=(shape(REDUN, LEAF), shape(RANK, RANK)),
        in_specs=vmem(2),
        out_specs=tuple(vmem(2)),
        name="leaf",
        cost_estimate=pl.CostEstimate(flops=2 * 10**9, bytes_accessed=3 * 2**20, transcendentals=0),
    )(diag_block[0], own_basis)

    half_count = blocks // 2
    near_offset = (near_index[0] - myself + half_count) % blocks - half_count
    far_offset = (far_index[0] - myself + half_count) % blocks - half_count
    columns = jnp.arange(3 * GROUP, dtype=jnp.int32)
    near_slots = jnp.arange(NEAR, dtype=jnp.int32)
    far_slots = NEAR + jnp.arange(FAR, dtype=jnp.int32)
    near_match = ((near_offset + GROUP + member)[:, None] == columns).astype(jnp.int32)
    far_match = ((far_offset + GROUP + member)[:, None] == columns).astype(jnp.int32)
    self_match = (columns == GROUP + member).astype(jnp.int32)
    source = (
        jnp.sum(near_match * near_slots[:, None], axis=0)
        + jnp.sum(far_match * far_slots[:, None], axis=0)
        + self_match * (NEAR + FAR)
    )
    children = jnp.arange(GROUP, dtype=jnp.int32)
    prev_rows = jnp.take(qskel_stack, children - GROUP - member + max_offset, axis=0)
    own_rows = jnp.take(complete_basis_stack, children - member + GROUP - 1, axis=0)
    next_rows = jnp.take(qskel_stack, children + GROUP - member + max_offset, axis=0)

    joined = pl.pallas_call(
        window_kernel,
        out_shape=shape(RANK, PAR + 2 * RANK),
        in_specs=[SMEM, SMEM] + vmem(8),
        out_specs=vmem(1)[0],
        scratch_shapes=[pltpu.VMEM((NEAR + FAR + 1, RANK, RANK), F32)],
        name="window",
    )(near_offset + max_offset, source, own_basis, near_blocks[0], far_coupling[0], leaf_schur, skel_stack, own_rows, prev_rows, next_rows)

    distances = list(range(1, GROUP)) + list(range(1 - GROUP, 0))
    gathered = {0: joined}
    for distance in distances:
        gathered[distance] = passed_along(joined, "blk", distance)
    stacked = jnp.stack([gathered[distance] for distance in range(1 - GROUP, GROUP)])
    all_v = jnp.take(stacked, member - children + GROUP - 1, axis=0)

    factor_rows, coupling_rows = pl.pallas_call(
        parent_kernel,
        out_shape=(shape(RANK, PRED), shape(RANK, PRED)),
        in_specs=[SMEM] + vmem(2),
        out_specs=tuple(vmem(2)),
        scratch_shapes=[
            pltpu.VMEM((PAR, PAR), BF16),
            pltpu.VMEM((PAR, PAR), BF16),
            pltpu.VMEM((PAR, PAR + 2 * RANK), BF16),
            pltpu.VMEM((PAR, PAR + 2 * RANK), BF16),
            pltpu.VMEM((PAR, PAR), F32),
            pltpu.VMEM((PAR + RANK, PRED), F32),
            pltpu.VMEM((PAR + RANK, PRED), BF16),
            pltpu.VMEM((PAR + RANK, PRED), BF16),
        ],
        name="parent",
    )(member[None], own_rows, all_v)
    return (leaf_out, factor_rows, coupling_rows)


def solution(mesh):
    placed = (
        P("blk", None, None),
        P("blk", None, None, None),
        P("blk", None, None, None),
        P("blk", None, None),
        P("blk", None),
        P("blk", None),
        P("blk", None),
    )
    return jax.shard_map(
        on_device,
        mesh=mesh,
        in_specs=placed,
        out_specs=(P("blk", None), P("blk", None), P("blk", None)),
        check_vma=False,
    )
```

time: 951 us -> 573 us (0.60)
  the two profiles are of different devices: /device:TPU:1 before, /device:TPU:88 now
where the time goes in v1:
time: 573 us; the launch traced here: 566 us
  waiting for transfers between devices  270 us (47%)
  local copies, waits for them, and re-layouts  130 us (23%)
  starting transfers between devices  80.5 us (14%)
  Pallas kernels  69 us (12%)
  other arithmetic  15.2 us (3%)
    ppermute x20, waiting for transfers between devices, passed_along(): return lax.ppermute(value, axis, pairs)  270 us
    ppermute x20, starting transfers between devices, passed_along(): return lax.ppermute(value, axis, pairs)  80.5 us
    unnamed x98, local copies, waits for them, and re-layouts  51.2 us
    pallas_call x1, Pallas kernels, on_device(): pl.pallas_call(parent_kernel, out_shape=(shape(RANK, PRED), shape(RANK, P...  39.1 us
    pallas_call x1, Pallas kernels, on_device(): pl.pallas_call(window_kernel, out_shape=shape(RANK, PAR + 2 * RANK), in_s...  19 us
    slice x12, local copies, waits for them, and re-layouts, split_close(): vector[LEAF * RANK:].reshape(RANK, PAR)  13.4 us
  transfers between devices with their start and end apart: 20, of which 14 were waited for; matrix products, arithmetic and copies ran while one was open for 10% of the time, Pallas kernels for 2%

profile of v1, /device:TPU:88, one launch (start us, length us, event | category | flops | bytes accessed | tf_op | source)
XLA Modules:
  0.0 566.0 jit_solution(8539560253997159788)
XLA Ops:
  5.1 1.7 collective-permute-start.11
  6.8 2.6 collective-permute-start.10
  9.5 1.4 copy.11
  11.9 7.8 %collective-permute-start.5 = (f32[393216]{0:T(1024)}, f32[393216]{0:T(1024)S(1)}, u32[]{:S(2)}, u32[]{:S(2)}) collective-permute-start(f32[393216]{0:T(1024)} %constant_dynamic-update-slice_fusion.30), channel_id=1, source_target_pairs={{0,253},{1,254},{2,255},{3,0},{4,1},{5,2},{6,3},{7,4},{8,5},{9,6},... | collective-permute-start | bytes 4718600 | tf_op jit(solution)/shard_map/ppermute | solution.py:197
  19.8 6.1 %collective-permute-done.13 = f32[196608]{0:T(1024)S(1)} collective-permute-done((f32[196608]{0:T(1024)}, f32[196608]{0:T(1024)S(1)}, u32[]{:S(2)}, u32[]{:S(2)}) %collective-permute-start.13) | collective-permute-done | bytes 786464 | tf_op jit(solution)/shard_map/ppermute | solution.py:197
  25.9 3.7 collective-permute-start.9
  29.7 27.1 %collective-permute-done.12 = f32[196608]{0:T(1024)} collective-permute-done((f32[196608]{0:T(1024)}, f32[196608]{0:T(1024)}, u32[]{:S(2)}, u32[]{:S(2)}) %collective-permute-start.12) | collective-permute-done | bytes 786464 | tf_op jit(solution)/shard_map/ppermute | solution.py:197
  56.8 8.7 %collective-permute-done.11 = f32[196608]{0:T(1024)} collective-permute-done((f32[196608]{0:T(1024)}, f32[196608]{0:T(1024)}, u32[]{:S(2)}, u32[]{:S(2)}) %collective-permute-start.11) | collective-permute-done | bytes 786464 | tf_op jit(solution)/shard_map/ppermute | solution.py:197
  65.5 7.2 %collective-permute-start.7 = (f32[196608]{0:T(1024)}, f32[196608]{0:T(1024)S(1)}, u32[]{:S(2)}, u32[]{:S(2)}) collective-permute-start(f32[196608]{0:T(1024)} %constant_dynamic-update-slice_fusion.31), channel_id=1, source_target_pairs={{0,6},{1,7},{2,8},{3,9},{4,10},{5,11},{6,12},{7,13},{8,14},{9,15},... | collective-permute-start | bytes 2359304 | tf_op jit(solution)/shard_map/ppermute | solution.py:197
  72.7 10.1 %collective-permute-done.10 = f32[196608]{0:T(1024)} collective-permute-done((f32[196608]{0:T(1024)}, f32[196608]{0:T(1024)}, u32[]{:S(2)}, u32[]{:S(2)}) %collective-permute-start.10) | collective-permute-done | bytes 786464 | tf_op jit(solution)/shard_map/ppermute | solution.py:197
  82.7 17.3 %collective-permute-start.6 = (f32[196608]{0:T(1024)}, f32[196608]{0:T(1024)}, u32[]{:S(2)}, u32[]{:S(2)}) collective-permute-start(f32[196608]{0:T(1024)} %constant_dynamic-update-slice_fusion.31), channel_id=1, source_target_pairs={{0,7},{1,8},{2,9},{3,10},{4,11},{5,12},{6,13},{7,14},{8,15},{9,16}... | collective-permute-start | bytes 2359304 | tf_op jit(solution)/shard_map/ppermute | solution.py:197
  100.1 10.9 %leaf.1 = (f32[256,512]{1,0:T(8,128)}, f32[256,256]{1,0:T(8,128)}) custom-call(f32[512,512]{1,0:T(8,128)} %bitcast.76, f32[512,512]{1,0:T(8,128)} %bitcast.69), custom_call_target="tpu_custom_call" | custom-call | flops 2000000000 | bytes 3145728 | tf_op jit(solution)/shard_map/leaf/pallas_call | solution.py:250
  111.1 13.0 %collective-permute-done.9 = f32[196608]{0:T(1024)} collective-permute-done((f32[196608]{0:T(1024)}, f32[196608]{0:T(1024)}, u32[]{:S(2)}, u32[]{:S(2)}) %collective-permute-start.9) | collective-permute-done | bytes 786464 | tf_op jit(solution)/shard_map/ppermute | solution.py:197
  124.1 72.6 %collective-permute-done.8 = f32[196608]{0:T(1024)S(1)} collective-permute-done((f32[196608]{0:T(1024)}, f32[196608]{0:T(1024)S(1)}, u32[]{:S(2)}, u32[]{:S(2)}) %collective-permute-start.8) | collective-permute-done | bytes 786464 | tf_op jit(solution)/shard_map/ppermute | solution.py:197
  196.7 2.5 collective-permute-done.7
  199.1 14.2 %collective-permute-start.2 = (f32[393216]{0:T(1024)}, f32[393216]{0:T(1024)}, u32[]{:S(2)}, u32[]{:S(2)}) collective-permute-start(f32[393216]{0:T(1024)} %constant_dynamic-update-slice_fusion.30), channel_id=1, source_target_pairs={{0,1},{1,2},{2,3},{3,4},{4,5},{5,6},{6,7},{7,8},{8,9},{9,10},{10,1... | collective-permute-start | bytes 4718600 | tf_op jit(solution)/shard_map/ppermute | solution.py:197
  238.1 1.7 constant_dynamic-update-slice_fusion.28
  256.9 10.9 %collective-permute-done.1 = f32[393216]{0:T(1024)} collective-permute-done((f32[393216]{0:T(1024)}, f32[393216]{0:T(1024)}, u32[]{:S(2)}, u32[]{:S(2)}) %collective-permute-start.1) | collective-permute-done | bytes 1572896 | tf_op jit(solution)/shard_map/ppermute | solution.py:197
  271.4 27.6 %collective-permute-done = f32[393216]{0:T(1024)} collective-permute-done((f32[393216]{0:T(1024)}, f32[393216]{0:T(1024)}, u32[]{:S(2)}, u32[]{:S(2)}) %collective-permute-start) | collective-permute-done | bytes 1572896 | tf_op jit(solution)/shard_map/ppermute | solution.py:197
  313.8 1.7 fusion.5
  315.4 1.7 fusion.4
  317.1 1.7 fusion.3
  319.5 1.7 fusion.2
  321.1 1.7 fusion.1
  322.8 1.7 fusion
  324.5 1.7 constant_dynamic-update-slice_fusion.25
  328.3 2.7 gather_fusion.3
  331.0 3.7 gather_fusion.2
  334.7 2.6 constant_dynamic-update-slice_fusion.6
  337.3 2.3 constant_dynamic-update-slice_fusion.5
  350.7 5.9 %gather_fusion = f32[4,256,1024]{2,1,0:T(8,128)} fusion(f32[7,256,1024]{2,1,0:T(8,128)} %constant_dynamic-update-slice_fusion.1, s32[1024]{0:T(1024)S(1)} %pad_clamp_fusion.3), kind=kCustom, calls=%fused_computation.2 | custom fusion | bytes 8388624 | tf_op jit(solution)/shard_map/jit(_take)/gather | solution.py:275
  356.6 5.2 broadcast_select_fusion.1.rows_ref
  367.8 19.0 %window.1 = f32[256,1536]{1,0:T(8,128)} custom-call(s32[6]{0:T(128)} %broadcast_add_fusion.index_ref, s32[12]{0:T(128)} %fusion.8.source_ref, f32[512,512]{1,0:T(8,128)} %bitcast.70, f32[6,512,512]{2,1,0:T(8,128)} %bitcast.67, f32[5,256,256]{2,1,0:T(8,128)} %bitcast.74, f32[256,256]{1,0:T(8,128)} %get-tuple-element.9.schur_ref, ...), custom_call_target="tpu_custom_call" | custom-call | tf_op jit(solution)/shard_map/window/pallas_call | solution.py:278
  386.8 5.9 %collective-permute-start.15 = (f32[256,1536]{1,0:T(8,128)}, f32[256,1536]{1,0:T(8,128)S(1)}, u32[]{:S(2)}, u32[]{:S(2)}) collective-permute-start(f32[256,1536]{1,0:T(8,128)} %window.1), channel_id=1, source_target_pairs={{0,254},{1,255},{2,0},{3,1},{4,2},{5,3},{6,4},{7,5},{8,6},{9,7},{1... | collective-permute-start | bytes 4718600 | tf_op jit(solution)/shard_map/ppermute | solution.py:197
  392.7 5.9 %collective-permute-start.16 = (f32[256,1536]{1,0:T(8,128)}, f32[256,1536]{1,0:T(8,128)S(1)}, u32[]{:S(2)}, u32[]{:S(2)}) collective-permute-start(f32[256,1536]{1,0:T(8,128)} %window.1), channel_id=1, source_target_pairs={{0,255},{1,0},{2,1},{3,2},{4,3},{5,4},{6,5},{7,6},{8,7},{9,8},{10,... | collective-permute-start | bytes 4718600 | tf_op jit(solution)/shard_map/ppermute | solution.py:197
  398.6 8.1 %collective-permute-start.19 = (f32[256,1536]{1,0:T(8,128)}, f32[256,1536]{1,0:T(8,128)S(1)}, u32[]{:S(2)}, u32[]{:S(2)}) collective-permute-start(f32[256,1536]{1,0:T(8,128)} %window.1), channel_id=1, source_target_pairs={{0,3},{1,4},{2,5},{3,6},{4,7},{5,8},{6,9},{7,10},{8,11},{9,12},{10... | collective-permute-start | bytes 4718600 | tf_op jit(solution)/shard_map/ppermute | solution.py:197
  406.7 2.1 collective-permute-start.18
  408.8 41.0 %collective-permute-done.14 = f32[256,1536]{1,0:T(8,128)S(1)} collective-permute-done((f32[256,1536]{1,0:T(8,128)}, f32[256,1536]{1,0:T(8,128)S(1)}, u32[]{:S(2)}, u32[]{:S(2)}) %collective-permute-start.14) | collective-permute-done | bytes 1572896 | tf_op jit(solution)/shard_map/ppermute | solution.py:197
  449.8 3.3 collective-permute-start.17
  454.4 4.1 collective-permute-done.15
  459.7 29.7 %collective-permute-done.16 = f32[256,1536]{1,0:T(8,128)S(1)} collective-permute-done((f32[256,1536]{1,0:T(8,128)}, f32[256,1536]{1,0:T(8,128)S(1)}, u32[]{:S(2)}, u32[]{:S(2)}) %collective-permute-start.16) | collective-permute-done | bytes 1572896 | tf_op jit(solution)/shard_map/ppermute | solution.py:197
  491.9 9.3 %collective-permute-done.17 = f32[256,1536]{1,0:T(8,128)S(1)} collective-permute-done((f32[256,1536]{1,0:T(8,128)}, f32[256,1536]{1,0:T(8,128)S(1)}, u32[]{:S(2)}, u32[]{:S(2)}) %collective-permute-start.17) | collective-permute-done | bytes 1572896 | tf_op jit(solution)/shard_map/ppermute | solution.py:197
  501.3 1.3 bitcast_dynamic-update-slice_fusion.2
  502.6 7.3 %collective-permute-done.18 = f32[256,1536]{1,0:T(8,128)S(1)} collective-permute-done((f32[256,1536]{1,0:T(8,128)}, f32[256,1536]{1,0:T(8,128)S(1)}, u32[]{:S(2)}, u32[]{:S(2)}) %collective-permute-start.18) | collective-permute-done | bytes 1572896 | tf_op jit(solution)/shard_map/ppermute | solution.py:197
  509.9 1.3 bitcast_dynamic-update-slice_fusion.1
  512.4 7.7 %gather_fusion.1 = f32[4,256,1536]{2,1,0:T(8,128)} fusion(f32[7,256,1536]{2,1,0:T(8,128)} %bitcast_dynamic-update-slice_fusion, s32[1024]{0:T(1024)S(1)} %pad_clamp_fusion), kind=kCustom, calls=%fused_computation.3 | custom fusion | bytes 12582928 | tf_op jit(solution)/shard_map/jit(_take)/gather | solution.py:292
  520.2 6.3 %broadcast_select_fusion.v_ref = f32[4,256,1536]{2,1,0:T(8,128)} fusion(f32[4,256,1536]{2,1,0:T(8,128)} %gather_fusion.1, pred[4]{0:T(512)(128)(4,1)S(1)} %compare_and_fusion.2), kind=kLoop, calls=%fused_computation.4 | loop fusion | flops 1572864 | bytes 12582916 | tf_op jit(solution)/shard_map/jit(_take)/select_n | solution.py:292
  526.4 39.1 %parent.1 = (f32[256,768]{1,0:T(8,128)}, f32[256,768]{1,0:T(8,128)}) custom-call(s32[1]{0:T(128)} %bitcast.2.member_ref, f32[4,256,1024]{2,1,0:T(8,128)} %broadcast_select_fusion.1.rows_ref, f32[4,256,1536]{2,1,0:T(8,128)} %broadcast_select_fusion.v_ref), custom_call_target="tpu_custom_call" | custom-call | tf_op jit(solution)/shard_map/parent/pallas_call | solution.py:294
  (188 shorter events, 91.9 us)
Async XLA Ops:
  0.6 99.4 %copy-start.24 = (s32[1,6]{1,0:T(1,128)S(1)}, s32[1,6]{1,0:T(1,128)}, u32[]{:S(2)}) copy-start(s32[1,6]{1,0:T(1,128)} %param.14) | copy-start | bytes 76
  4.2 106.9 %copy-start.25 = (s32[1,5]{1,0:T(1,128)S(1)}, s32[1,5]{1,0:T(1,128)}, u32[]{:S(2)}) copy-start(s32[1,5]{1,0:T(1,128)} %param.15) | copy-start | bytes 64
  4.9 21.0 %collective-permute-start.13 = (f32[196608]{0:T(1024)}, f32[196608]{0:T(1024)S(1)}, u32[]{:S(2)}, u32[]{:S(2)}) collective-permute-start(f32[196608]{0:T(1024)} %constant_dynamic-update-slice_fusion.31), channel_id=1, source_target_pairs={{0,249},{1,250},{2,251},{3,252},{4,253},{5,254},{6,255},{7,0},{8,1... | collective-permute-start | bytes 2359304 | tf_op jit(solution)/shard_map/ppermute | solution.py:197
  4.9 51.9 %collective-permute-start.12 = (f32[196608]{0:T(1024)}, f32[196608]{0:T(1024)}, u32[]{:S(2)}, u32[]{:S(2)}) collective-permute-start(f32[196608]{0:T(1024)} %constant_dynamic-update-slice_fusion.31), channel_id=1, source_target_pairs={{0,250},{1,251},{2,252},{3,253},{4,254},{5,255},{6,0},{7,1},{8,2},... | collective-permute-start | bytes 2359304 | tf_op jit(solution)/shard_map/ppermute | solution.py:197
  5.1 60.4 %collective-permute-start.11 = (f32[196608]{0:T(1024)}, f32[196608]{0:T(1024)}, u32[]{:S(2)}, u32[]{:S(2)}) collective-permute-start(f32[196608]{0:T(1024)} %constant_dynamic-update-slice_fusion.31), channel_id=1, source_target_pairs={{0,251},{1,252},{2,253},{3,254},{4,255},{5,0},{6,1},{7,2},{8,3},{9... | collective-permute-start | bytes 2359304 | tf_op jit(solution)/shard_map/ppermute | solution.py:197
  6.8 75.9 %collective-permute-start.10 = (f32[196608]{0:T(1024)}, f32[196608]{0:T(1024)}, u32[]{:S(2)}, u32[]{:S(2)}) collective-permute-start(f32[196608]{0:T(1024)} %constant_dynamic-update-slice_fusion.31), channel_id=1, source_target_pairs={{0,252},{1,253},{2,254},{3,255},{4,0},{5,1},{6,2},{7,3},{8,4},{9,5... | collective-permute-start | bytes 2359304 | tf_op jit(solution)/shard_map/ppermute | solution.py:197
  11.9 201.4 %collective-permute-start.5 = (f32[393216]{0:T(1024)}, f32[393216]{0:T(1024)S(1)}, u32[]{:S(2)}, u32[]{:S(2)}) collective-permute-start(f32[393216]{0:T(1024)} %constant_dynamic-update-slice_fusion.30), channel_id=1, source_target_pairs={{0,253},{1,254},{2,255},{3,0},{4,1},{5,2},{6,3},{7,4},{8,5},{9,6},... | collective-permute-start | bytes 4718600 | tf_op jit(solution)/shard_map/ppermute | solution.py:197
  25.9 98.1 %collective-permute-start.9 = (f32[196608]{0:T(1024)}, f32[196608]{0:T(1024)}, u32[]{:S(2)}, u32[]{:S(2)}) collective-permute-start(f32[196608]{0:T(1024)} %constant_dynamic-update-slice_fusion.31), channel_id=1, source_target_pairs={{0,4},{1,5},{2,6},{3,7},{4,8},{5,9},{6,10},{7,11},{8,12},{9,13},{1... | collective-permute-start | bytes 2359304 | tf_op jit(solution)/shard_map/ppermute | solution.py:197
  56.8 139.9 %collective-permute-start.8 = (f32[196608]{0:T(1024)}, f32[196608]{0:T(1024)S(1)}, u32[]{:S(2)}, u32[]{:S(2)}) collective-permute-start(f32[196608]{0:T(1024)} %constant_dynamic-update-slice_fusion.31), channel_id=1, source_target_pairs={{0,5},{1,6},{2,7},{3,8},{4,9},{5,10},{6,11},{7,12},{8,13},{9,14},{... | collective-permute-start | bytes 2359304 | tf_op jit(solution)/shard_map/ppermute | solution.py:197
  65.5 133.6 %collective-permute-start.7 = (f32[196608]{0:T(1024)}, f32[196608]{0:T(1024)S(1)}, u32[]{:S(2)}, u32[]{:S(2)}) collective-permute-start(f32[196608]{0:T(1024)} %constant_dynamic-update-slice_fusion.31), channel_id=1, source_target_pairs={{0,6},{1,7},{2,8},{3,9},{4,10},{5,11},{6,12},{7,13},{8,14},{9,15},... | collective-permute-start | bytes 2359304 | tf_op jit(solution)/shard_map/ppermute | solution.py:197
  82.7 130.6 %collective-permute-start.6 = (f32[196608]{0:T(1024)}, f32[196608]{0:T(1024)}, u32[]{:S(2)}, u32[]{:S(2)}) collective-permute-start(f32[196608]{0:T(1024)} %constant_dynamic-update-slice_fusion.31), channel_id=1, source_target_pairs={{0,7},{1,8},{2,9},{3,10},{4,11},{5,12},{6,13},{7,14},{8,15},{9,16}... | collective-permute-start | bytes 2359304 | tf_op jit(solution)/shard_map/ppermute | solution.py:197
  124.1 122.9 %collective-permute-start.4 = (f32[393216]{0:T(1024)}, f32[393216]{0:T(1024)}, u32[]{:S(2)}, u32[]{:S(2)}) collective-permute-start(f32[393216]{0:T(1024)} %constant_dynamic-update-slice_fusion.30), channel_id=1, source_target_pairs={{0,254},{1,255},{2,0},{3,1},{4,2},{5,3},{6,4},{7,5},{8,6},{9,7},{1... | collective-permute-start | bytes 4718600 | tf_op jit(solution)/shard_map/ppermute | solution.py:197
  196.7 17.8 %copy-start.21 = (f32[196608]{0:T(1024)}, f32[196608]{0:T(1024)S(1)}, u32[]{:S(2)}) copy-start(f32[196608]{0:T(1024)S(1)} %collective-permute-done.8) | copy-start | bytes 2359300
  196.7 54.0 %collective-permute-start.3 = (f32[393216]{0:T(1024)}, f32[393216]{0:T(1024)}, u32[]{:S(2)}, u32[]{:S(2)}) collective-permute-start(f32[393216]{0:T(1024)} %constant_dynamic-update-slice_fusion.30), channel_id=1, source_target_pairs={{0,255},{1,0},{2,1},{3,2},{4,3},{5,4},{6,5},{7,6},{8,7},{9,8},{10,... | collective-permute-start | bytes 4718600 | tf_op jit(solution)/shard_map/ppermute | solution.py:197
  199.1 30.3 %copy-start.22 = (f32[196608]{0:T(1024)}, f32[196608]{0:T(1024)S(1)}, u32[]{:S(2)}) copy-start(f32[196608]{0:T(1024)S(1)} %collective-permute-done.7) | copy-start | bytes 2359300
  199.1 55.1 %collective-permute-start.2 = (f32[393216]{0:T(1024)}, f32[393216]{0:T(1024)}, u32[]{:S(2)}, u32[]{:S(2)}) collective-permute-start(f32[393216]{0:T(1024)} %constant_dynamic-update-slice_fusion.30), channel_id=1, source_target_pairs={{0,1},{1,2},{2,3},{3,4},{4,5},{5,6},{6,7},{7,8},{8,9},{9,10},{10,1... | collective-permute-start | bytes 4718600 | tf_op jit(solution)/shard_map/ppermute | solution.py:197
  213.3 54.4 %collective-permute-start.1 = (f32[393216]{0:T(1024)}, f32[393216]{0:T(1024)}, u32[]{:S(2)}, u32[]{:S(2)}) collective-permute-start(f32[393216]{0:T(1024)} %constant_dynamic-update-slice_fusion.30), channel_id=1, source_target_pairs={{0,2},{1,3},{2,4},{3,5},{4,6},{5,7},{6,8},{7,9},{8,10},{9,11},{10,... | collective-permute-start | bytes 4718600 | tf_op jit(solution)/shard_map/ppermute | solution.py:197
  213.3 16.1 %copy-start.17 = (f32[393216]{0:T(1024)}, f32[393216]{0:T(1024)S(1)}, u32[]{:S(2)}) copy-start(f32[393216]{0:T(1024)S(1)} %collective-permute-done.5) | copy-start | bytes 4718596
  213.3 85.6 %collective-permute-start = (f32[393216]{0:T(1024)}, f32[393216]{0:T(1024)}, u32[]{:S(2)}, u32[]{:S(2)}) collective-permute-start(f32[393216]{0:T(1024)} %constant_dynamic-update-slice_fusion.30), channel_id=1, source_target_pairs={{0,3},{1,4},{2,5},{3,6},{4,7},{5,8},{6,9},{7,10},{8,11},{9,12},{10... | collective-permute-start | bytes 4718600 | tf_op jit(solution)/shard_map/ppermute | solution.py:197
  221.1 11.9 %slice-start.1 = ((f32[196608]{0:T(1024)}), f32[65536]{0:T(1024)S(1)}, s32[]{:S(2)}) async-start(f32[196608]{0:T(1024)} %copy-done.21), calls=%async_computation.1 | async-start | bytes 524288 | tf_op jit(solution)/shard_map/slice | solution.py:205
  230.6 3.8 slice-start.2
  237.4 7.2 %copy-start.18 = (f32[393216]{0:T(1024)S(1)}, f32[393216]{0:T(1024)}, u32[]{:S(2)}) copy-start(f32[393216]{0:T(1024)} %copy-done.17) | copy-start | bytes 4718596
  269.1 33.5 %slice-start = ((f32[393216]{0:T(1024)}), f32[131072]{0:T(1024)S(1)}, s32[]{:S(2)}) async-start(f32[393216]{0:T(1024)} %copy-done.17), calls=%async_computation | async-start | bytes 1048576 | tf_op jit(solution)/shard_map/slice | solution.py:201
  303.5 15.2 %copy-start = (f32[256,1024]{1,0:T(8,128)S(1)}, f32[256,1024]{1,0:T(8,128)}, u32[]{:S(2)}) copy-start(f32[256,1024]{1,0:T(8,128)} %param.13) | copy-start | bytes 3145732
  305.6 20.5 %copy-start.20 = (f32[1,256,256]{2,1,0:T(8,128)S(1)}, f32[1,256,256]{2,1,0:T(8,128)}, u32[]{:S(2)}) copy-start(f32[1,256,256]{2,1,0:T(8,128)} %slice.360) | copy-start | bytes 786436
  306.8 20.1 %copy-start.19 = (f32[1,256,256]{2,1,0:T(8,128)S(1)}, f32[1,256,256]{2,1,0:T(8,128)}, u32[]{:S(2)}) copy-start(f32[1,256,256]{2,1,0:T(8,128)} %slice.362) | copy-start | bytes 786436
  334.7 7.0 %copy-start.16 = (f32[1,512,256]{2,1,0:T(8,128)S(1)}, f32[1,512,256]{2,1,0:T(8,128)}, u32[]{:S(2)}) copy-start(f32[1,512,256]{2,1,0:T(8,128)} %slice.322) | copy-start | bytes 1572868
  334.7 7.9 %copy-start.15 = (f32[1,512,256]{2,1,0:T(8,128)S(1)}, f32[1,512,256]{2,1,0:T(8,128)}, u32[]{:S(2)}) copy-start(f32[1,512,256]{2,1,0:T(8,128)} %slice.324) | copy-start | bytes 1572868
  334.7 8.7 %copy-start.14 = (f32[1,512,256]{2,1,0:T(8,128)S(1)}, f32[1,512,256]{2,1,0:T(8,128)}, u32[]{:S(2)}) copy-start(f32[1,512,256]{2,1,0:T(8,128)} %slice.326) | copy-start | bytes 1572868
  334.7 9.5 %copy-start.2 = (f32[1,512,512]{2,1,0:T(8,128)S(1)}, f32[1,512,512]{2,1,0:T(8,128)}, u32[]{:S(2)}) copy-start(f32[1,512,512]{2,1,0:T(8,128)} %param.12) | copy-start | bytes 3145732
  334.7 10.3 %copy-start.3 = (f32[4,256,256]{2,1,0:T(8,128)S(1)}, f32[4,256,256]{2,1,0:T(8,128)}, u32[]{:S(2)}) copy-start(f32[4,256,256]{2,1,0:T(8,128)} %gather_fusion.2) | copy-start | bytes 3145732
  339.6 7.7 %copy-start.6 = (f32[1,256,1024]{2,1,0:T(8,128)S(1)}, f32[1,256,1024]{2,1,0:T(8,128)}, u32[]{:S(2)}) copy-start(f32[1,256,1024]{2,1,0:T(8,128)} %stack_reshape.59) | copy-start | bytes 3145732
  340.7 7.8 %copy-start.5 = (f32[1,256,1024]{2,1,0:T(8,128)S(1)}, f32[1,256,1024]{2,1,0:T(8,128)}, u32[]{:S(2)}) copy-start(f32[1,256,1024]{2,1,0:T(8,128)} %stack_reshape.60) | copy-start | bytes 3145732
  341.7 7.9 %copy-start.4 = (f32[1,256,1024]{2,1,0:T(8,128)S(1)}, f32[1,256,1024]{2,1,0:T(8,128)}, u32[]{:S(2)}) copy-start(f32[1,256,1024]{2,1,0:T(8,128)} %stack_reshape.61) | copy-start | bytes 3145732
  356.6 5.3 copy-start.13
  356.6 6.1 %copy-start.12 = (f32[1,512,256]{2,1,0:T(8,128)S(1)}, f32[1,512,256]{2,1,0:T(8,128)}, u32[]{:S(2)}) copy-start(f32[1,512,256]{2,1,0:T(8,128)} %slice.330) | copy-start | bytes 1572868
  356.6 7.0 %copy-start.11 = (f32[1,512,256]{2,1,0:T(8,128)S(1)}, f32[1,512,256]{2,1,0:T(8,128)}, u32[]{:S(2)}) copy-start(f32[1,512,256]{2,1,0:T(8,128)} %slice.332) | copy-start | bytes 1572868
  356.6 7.8 %copy-start.10 = (f32[1,512,256]{2,1,0:T(8,128)S(1)}, f32[1,512,256]{2,1,0:T(8,128)}, u32[]{:S(2)}) copy-start(f32[1,512,256]{2,1,0:T(8,128)} %stack_reshape.66) | copy-start | bytes 1572868
  356.6 8.6 %copy-start.9 = (f32[1,512,256]{2,1,0:T(8,128)S(1)}, f32[1,512,256]{2,1,0:T(8,128)}, u32[]{:S(2)}) copy-start(f32[1,512,256]{2,1,0:T(8,128)} %stack_reshape.67) | copy-start | bytes 1572868
  356.6 9.4 %copy-start.8 = (f32[1,512,256]{2,1,0:T(8,128)S(1)}, f32[1,512,256]{2,1,0:T(8,128)}, u32[]{:S(2)}) copy-start(f32[1,512,256]{2,1,0:T(8,128)} %stack_reshape.68) | copy-start | bytes 1572868
  356.6 10.3 %copy-start.7 = (f32[1,512,256]{2,1,0:T(8,128)S(1)}, f32[1,512,256]{2,1,0:T(8,128)}, u32[]{:S(2)}) copy-start(f32[1,512,256]{2,1,0:T(8,128)} %stack_reshape.69) | copy-start | bytes 1572868
  386.8 103.9 %copy-start.1 = (f32[256,1536]{1,0:T(8,128)S(1)}, f32[256,1536]{1,0:T(8,128)}, u32[]{:S(2)}) copy-start(f32[256,1536]{1,0:T(8,128)} %window.1) | copy-start | bytes 4718596
  386.8 63.0 %collective-permute-start.14 = (f32[256,1536]{1,0:T(8,128)}, f32[256,1536]{1,0:T(8,128)S(1)}, u32[]{:S(2)}, u32[]{:S(2)}) collective-permute-start(f32[256,1536]{1,0:T(8,128)} %window.1), channel_id=1, source_target_pairs={{0,253},{1,254},{2,255},{3,0},{4,1},{5,2},{6,3},{7,4},{8,5},{9,6},... | collective-permute-start | bytes 4718600 | tf_op jit(solution)/shard_map/ppermute | solution.py:197
  386.8 71.6 %collective-permute-start.15 = (f32[256,1536]{1,0:T(8,128)}, f32[256,1536]{1,0:T(8,128)S(1)}, u32[]{:S(2)}, u32[]{:S(2)}) collective-permute-start(f32[256,1536]{1,0:T(8,128)} %window.1), channel_id=1, source_target_pairs={{0,254},{1,255},{2,0},{3,1},{4,2},{5,3},{6,4},{7,5},{8,6},{9,7},{1... | collective-permute-start | bytes 4718600 | tf_op jit(solution)/shard_map/ppermute | solution.py:197
  392.7 96.7 %collective-permute-start.16 = (f32[256,1536]{1,0:T(8,128)}, f32[256,1536]{1,0:T(8,128)S(1)}, u32[]{:S(2)}, u32[]{:S(2)}) collective-permute-start(f32[256,1536]{1,0:T(8,128)} %window.1), channel_id=1, source_target_pairs={{0,255},{1,0},{2,1},{3,2},{4,3},{5,4},{6,5},{7,6},{8,7},{9,8},{10,... | collective-permute-start | bytes 4718600 | tf_op jit(solution)/shard_map/ppermute | solution.py:197
  398.6 112.6 %collective-permute-start.19 = (f32[256,1536]{1,0:T(8,128)}, f32[256,1536]{1,0:T(8,128)S(1)}, u32[]{:S(2)}, u32[]{:S(2)}) collective-permute-start(f32[256,1536]{1,0:T(8,128)} %window.1), channel_id=1, source_target_pairs={{0,3},{1,4},{2,5},{3,6},{4,7},{5,8},{6,9},{7,10},{8,11},{9,12},{10... | collective-permute-start | bytes 4718600 | tf_op jit(solution)/shard_map/ppermute | solution.py:197
  406.7 103.1 %collective-permute-start.18 = (f32[256,1536]{1,0:T(8,128)}, f32[256,1536]{1,0:T(8,128)S(1)}, u32[]{:S(2)}, u32[]{:S(2)}) collective-permute-start(f32[256,1536]{1,0:T(8,128)} %window.1), channel_id=1, source_target_pairs={{0,2},{1,3},{2,4},{3,5},{4,6},{5,7},{6,8},{7,9},{8,10},{9,11},{10,... | collective-permute-start | bytes 4718600 | tf_op jit(solution)/shard_map/ppermute | solution.py:197
  449.8 51.5 %collective-permute-start.17 = (f32[256,1536]{1,0:T(8,128)}, f32[256,1536]{1,0:T(8,128)S(1)}, u32[]{:S(2)}, u32[]{:S(2)}) collective-permute-start(f32[256,1536]{1,0:T(8,128)} %window.1), channel_id=1, source_target_pairs={{0,1},{1,2},{2,3},{3,4},{4,5},{5,6},{6,7},{7,8},{8,9},{9,10},{10,1... | collective-permute-start | bytes 4718600 | tf_op jit(solution)/shard_map/ppermute | solution.py:197
  (1 other events, 3.7 us)

commit v2 on v1

--- a/solution.py
+++ b/solution.py
@@ -19,6 +19,7 @@
 NN = (((1,), (0,)), ((), ()))
 NT = (((1,), (1,)), ((), ()))
 TN = (((0,), (0,)), ((), ()))
+MESH = pl.DeviceIdType.MESH
 
 
 def split2(x):
@@ -110,33 +111,158 @@
     schur_ref[...] = corner - dot_split(coupled, coupled, TN)
 
 
-def window_kernel(index_ref, source_ref, basis_ref, near_ref, far_ref, schur_ref, skel_ref, rows_ref, prev_ref, next_ref, out_ref, blocks):
-    skeleton = split2(basis_ref[:, REDUN:])
+def exchange_kernel(kind_ref, near_at_ref, far_at_ref, basis_ref, near_ref, far_ref, schur_ref, parent_ref, rows_ref, v_ref, skel, sides, near, far, left_hi, left_lo, h_hi, h_lo, local_sem, send_sem, recv_sem):
+    me = lax.axis_index("blk")
+    count = lax.axis_size("blk")
+    core = lax.rem(me, 2)
+    member = lax.rem(me, GROUP)
+    y = lax.rem(lax.div(me, 2), 4)
+    upper = lax.div(y, 2)
+    other = lax.rem(member + 2, GROUP)
+    partner = me + 1 - 2 * core
+    sibling = me + 2 - 4 * lax.rem(y, 2)
+    across = me + 2 * (3 - 2 * y)
+    step = 8 - 16 * upper
+    onward = lax.rem(me + step + count, count)
+    behind = lax.rem(me - step + count, count)
+    near_side, far_side = 2 - 2 * upper, 2 * upper
+
+    def rows_of(child):
+        return pl.ds(pl.multiple_of(child * RANK, RANK), RANK)
+
+    mine = rows_of(member)
+    left_cols, skel_cols = pl.ds(0, PRED), pl.ds(PRED, RANK)
+    local = [
+        pltpu.make_async_copy(basis_ref.at[:, pl.ds(REDUN, RANK)], skel.at[1, member], local_sem.at[0]),
+        pltpu.make_async_copy(near_ref, near, local_sem.at[1]),
+        pltpu.make_async_copy(parent_ref, rows_ref.at[mine, :], local_sem.at[2]),
+        pltpu.make_async_copy(far_ref, far, local_sem.at[3]),
+    ]
+    for copy in local:
+        copy.start()
+
+    barrier = pltpu.get_barrier_semaphore()
+    for device in (partner, sibling, across, onward, behind):
+        pl.semaphore_signal(barrier, inc=1, device_id=(device,), device_id_type=MESH)
+    pl.semaphore_wait(barrier, 5)
+
+    started = []
+
+    def send(src, dst, device):
+        at = len(started)
+        copy = pltpu.make_async_remote_copy(
+            src_ref=src, dst_ref=dst, send_sem=send_sem.at[at], recv_sem=recv_sem.at[at], device_id=(device,), device_id_type=MESH
+        )
+        copy.start()
+        started.append(copy)
+        return copy
+
+    def send_same(ref, device):
+        return send(ref, ref, device)
+
+    own_skel = basis_ref.at[:, pl.ds(REDUN, RANK)]
+    own_side = parent_ref.at[:, skel_cols]
+    sib_s = send(own_skel, skel.at[1, member], sibling)
+    cross_s = send(own_skel, skel.at[far_side, member], across)
+    pair_s = send(own_skel, skel.at[1, member], partner)
+    sib_p = send(own_side, rows_ref.at[mine, skel_cols], sibling)
+    cross_p = send(own_side, sides.at[upper, mine, :], across)
+    pair_p = send(parent_ref, rows_ref.at[mine, :], partner)
+    sib_r = send(parent_ref.at[:, left_cols], rows_ref.at[mine, left_cols], sibling)
+
+    local[0].wait()
+    local[1].wait()
+    own = split2(skel[1, member].T)
 
     def one_near(slot, carry):
-        left = dot_split(skeleton, split2(near_ref[slot]), TN)
-        blocks[slot] = dot3(left, skel_ref[index_ref[slot]], NN)
+        left_hi[slot], left_lo[slot] = split2(dot_split(own, split2(near[slot]), NN))
         return carry
 
     lax.fori_loop(0, NEAR, one_near, 0)
-    for slot in range(FAR):
-        blocks[NEAR + slot] = far_ref[slot]
-    blocks[NEAR + FAR] = schur_ref[...]
-
-    def term(column, rows):
-        return dot3(blocks[source_ref[column]], rows, NN)
-
-    for half in range(2):
-        cols = slice(half * 512, half * 512 + 512)
-        total = term(GROUP, rows_ref[0][:, cols])
-        for child in range(1, GROUP):
-            total += term(GROUP + child, rows_ref[child][:, cols])
-        out_ref[:, cols] = total
-    for base, ref, at in ((0, prev_ref, PAR), (2 * GROUP, next_ref, PAR + RANK)):
-        total = term(base, ref[0])
-        for child in range(1, GROUP):
-            total += term(base + child, ref[child])
-        out_ref[:, at : at + RANK] = total
+    theirs = rows_of(other)
+    sib_s.wait_recv()
+    relay_s = send(skel.at[1, other], skel.at[far_side, other], across)
+    pair_sib_s = send_same(skel.at[1, other], partner)
+    cross_s.wait_recv()
+    on_s = send(skel.at[near_side, other], skel.at[far_side, other], onward)
+    pair_cross_s = send_same(skel.at[near_side, other], partner)
+    sib_p.wait_recv()
+    relay_p = send(rows_ref.at[theirs, skel_cols], sides.at[upper, theirs, :], across)
+    cross_p.wait_recv()
+    on_p = send(sides.at[1 - upper, theirs, :], sides.at[upper, theirs, :], onward)
+    pair_cross_p = send_same(sides.at[1 - upper, theirs, :], partner)
+    relay_s.wait_recv()
+    on_relay_s = send(skel.at[near_side, member], skel.at[far_side, member], onward)
+    pair_relay_s = send_same(skel.at[near_side, member], partner)
+    on_s.wait_recv()
+    pair_on_s = send_same(skel.at[far_side, other], partner)
+    relay_p.wait_recv()
+    on_relay_p = send(sides.at[1 - upper, mine, :], sides.at[upper, mine, :], onward)
+    pair_relay_p = send_same(sides.at[1 - upper, mine, :], partner)
+    on_p.wait_recv()
+    pair_on_p = send_same(sides.at[upper, theirs, :], partner)
+    sib_r.wait_recv()
+    pair_sib_p = send_same(rows_ref.at[theirs, :], partner)
+    local[2].wait()
+    local[3].wait()
+
+    def fill(side):
+        def one(child, carry):
+            column = side * GROUP + child
+            left = (left_hi[near_at_ref[column]], left_lo[near_at_ref[column]])
+            block = dot_split(left, split2(skel[side, child]), NN)
+            block = jnp.where(kind_ref[column] == 1, block, far[far_at_ref[column]])
+            block = jnp.where((column == GROUP + member), schur_ref[...], block)
+            at = rows_of(child)
+            h_hi[:, at], h_lo[:, at] = split2(block)
+            return carry
+
+        lax.fori_loop(0, GROUP, one, 0)
+        return h_hi[...], h_lo[...]
+
+    pair_s.wait_recv()
+    pair_sib_s.wait_recv()
+    pair_p.wait_recv()
+    h_own = fill(1)
+    pair_sib_p.wait_recv()
+    v_pairs, v_sibs = [], []
+    for part in range(2):
+        cols = pl.ds(part * 512, 512)
+        v_ref[mine, cols] = dot_split(h_own, split2(rows_ref[:, cols]), NN)
+        v_sibs.append(send_same(v_ref.at[mine, cols], sibling))
+        v_pairs.append(send_same(v_ref.at[mine, cols], partner))
+    pair_cross_s.wait_recv()
+    pair_cross_p.wait_recv()
+    pair_relay_s.wait_recv()
+    pair_relay_p.wait_recv()
+
+    def side_product(side, at):
+        v_ref[mine, pl.ds(PAR + pl.multiple_of(at * RANK, RANK), RANK)] = dot_split(fill(side), split2(sides[at]), NN)
+
+    side_product(near_side, 1 - upper)
+    on_relay_s.wait_recv()
+    pair_on_relay_s = send_same(skel.at[far_side, member], partner)
+    on_relay_p.wait_recv()
+    pair_on_relay_p = send_same(sides.at[upper, mine, :], partner)
+    pair_on_s.wait_recv()
+    pair_on_p.wait_recv()
+    pair_on_relay_s.wait_recv()
+    pair_on_relay_p.wait_recv()
+    side_product(far_side, upper)
+    cols = pl.ds(PAR, 2 * RANK)
+    v_sibs.append(send_same(v_ref.at[mine, cols], sibling))
+    v_pairs.append(send_same(v_ref.at[mine, cols], partner))
+    passed = []
+    for part in range(3):
+        v_sibs[part].wait_recv()
+        passed.append(send_same(v_ref.at[theirs, pl.ds(part * 512, 512)], partner))
+    for copy in v_pairs + passed:
+        copy.wait_recv()
+    for copy in started:
+        copy.wait_send()
+
+
+COPIES = 32
 
 
 def parent_kernel(member_ref, rows_ref, v_ref, factor_ref, couple_ref, basis_hi, basis_lo, v_hi, v_lo, c_ref, low_ref, low_hi, low_lo):
@@ -144,8 +270,8 @@
     rows = PAR + RANK
     for child in range(GROUP):
         at = slice(child * RANK, child * RANK + RANK)
-        basis_hi[at, :], basis_lo[at, :] = split2(rows_ref[child])
-        v_hi[at, :], v_lo[at, :] = split2(v_ref[child])
+        basis_hi[at, :], basis_lo[at, :] = split2(rows_ref[at, :])
+        v_hi[at, :], v_lo[at, :] = split2(v_ref[at, :])
 
     def piece(step, carry):
         at = pl.ds(pl.multiple_of(step * RANK, RANK), RANK)
@@ -191,20 +317,6 @@
         couple_ref[:, RANK : 2 * RANK] = c_ref[PRED:, PRED:] - dot_split(left, right, NT)
 
 
-def passed_along(value, axis, steps):
-    count = lax.axis_size(axis)
-    pairs = [(source, (source + steps) % count) for source in range(count)]
-    return lax.ppermute(value, axis, pairs)
-
-
-def split_close(vector):
-    return (vector[: LEAF * RANK].reshape(LEAF, RANK), vector[LEAF * RANK :].reshape(RANK, PAR))
-
-
-def split_far(vector):
-    return (vector[: LEAF * RANK].reshape(LEAF, RANK), vector[LEAF * RANK :].reshape(RANK, RANK))
-
-
 def shape(*dims):
     return jax.ShapeDtypeStruct(dims, F32)
 
@@ -220,33 +332,7 @@
     blocks = lax.axis_size("blk")
     myself = lax.axis_index("blk")
     member = myself % GROUP
-    max_offset = 2 * GROUP - 1
     own_basis = leaf_basis[0]
-    skeleton = own_basis[:, REDUN:]
-    close_load = jnp.concatenate([skeleton.reshape(-1), parent_basis.reshape(-1)])
-    far_load = jnp.concatenate([skeleton.reshape(-1), parent_basis[:, PRED:].reshape(-1)])
-    received = {0: close_load}
-    for offset in range(-max_offset, max_offset + 1):
-        if 0 < abs(offset) < GROUP:
-            received[offset] = passed_along(close_load, "blk", -offset)
-        elif abs(offset) >= GROUP:
-            received[offset] = passed_along(far_load, "blk", -offset)
-    skel_list = []
-    qskel_list = []
-    qfull_list = []
-    for offset in range(-max_offset, max_offset + 1):
-        if abs(offset) < GROUP:
-            skel_part, row_block = split_close(received[offset])
-            qfull_list.append(row_block)
-            qskel_list.append(row_block[:, PRED:])
-        else:
-            skel_part, row_block = split_far(received[offset])
-            qskel_list.append(row_block)
-        skel_list.append(skel_part)
-    skel_stack = jnp.stack(skel_list)
-    qskel_stack = jnp.stack(qskel_list)
-    complete_basis_stack = jnp.stack(qfull_list)
-
     leaf_out, leaf_schur = pl.pallas_call(
         leaf_kernel,
         out_shape=(shape(REDUN, LEAF), shape(RANK, RANK)),
@@ -256,40 +342,35 @@
         cost_estimate=pl.CostEstimate(flops=2 * 10**9, bytes_accessed=3 * 2**20, transcendentals=0),
     )(diag_block[0], own_basis)
 
-    half_count = blocks // 2
-    near_offset = (near_index[0] - myself + half_count) % blocks - half_count
-    far_offset = (far_index[0] - myself + half_count) % blocks - half_count
+    start = GROUP * (myself // GROUP - 1)
     columns = jnp.arange(3 * GROUP, dtype=jnp.int32)
-    near_slots = jnp.arange(NEAR, dtype=jnp.int32)
-    far_slots = NEAR + jnp.arange(FAR, dtype=jnp.int32)
-    near_match = ((near_offset + GROUP + member)[:, None] == columns).astype(jnp.int32)
-    far_match = ((far_offset + GROUP + member)[:, None] == columns).astype(jnp.int32)
-    self_match = (columns == GROUP + member).astype(jnp.int32)
-    source = (
-        jnp.sum(near_match * near_slots[:, None], axis=0)
-        + jnp.sum(far_match * far_slots[:, None], axis=0)
-        + self_match * (NEAR + FAR)
-    )
-    children = jnp.arange(GROUP, dtype=jnp.int32)
-    prev_rows = jnp.take(qskel_stack, children - GROUP - member + max_offset, axis=0)
-    own_rows = jnp.take(complete_basis_stack, children - member + GROUP - 1, axis=0)
-    next_rows = jnp.take(qskel_stack, children + GROUP - member + max_offset, axis=0)
-
-    joined = pl.pallas_call(
-        window_kernel,
-        out_shape=shape(RANK, PAR + 2 * RANK),
-        in_specs=[SMEM, SMEM] + vmem(8),
-        out_specs=vmem(1)[0],
-        scratch_shapes=[pltpu.VMEM((NEAR + FAR + 1, RANK, RANK), F32)],
-        name="window",
-    )(near_offset + max_offset, source, own_basis, near_blocks[0], far_coupling[0], leaf_schur, skel_stack, own_rows, prev_rows, next_rows)
-
-    distances = list(range(1, GROUP)) + list(range(1 - GROUP, 0))
-    gathered = {0: joined}
-    for distance in distances:
-        gathered[distance] = passed_along(joined, "blk", distance)
-    stacked = jnp.stack([gathered[distance] for distance in range(1 - GROUP, GROUP)])
-    all_v = jnp.take(stacked, member - children + GROUP - 1, axis=0)
+    near_match = ((near_index[0] - start + blocks) % blocks)[:, None] == columns
+    far_match = ((far_index[0] - start + blocks) % blocks)[:, None] == columns
+    near_at = jnp.sum(near_match * jnp.arange(NEAR, dtype=jnp.int32)[:, None], axis=0)
+    far_at = jnp.sum(far_match * jnp.arange(FAR, dtype=jnp.int32)[:, None], axis=0)
+    kind = jnp.sum(near_match.astype(jnp.int32), axis=0)
+    anywhere = [pl.BlockSpec(memory_space=pl.ANY)]
+    all_rows, all_v = pl.pallas_call(
+        exchange_kernel,
+        out_shape=(shape(PAR, PAR), shape(PAR, PAR + 2 * RANK)),
+        in_specs=[SMEM] * 3 + anywhere * 3 + vmem(1) + anywhere,
+        out_specs=tuple(vmem(2)),
+        scratch_shapes=[
+            pltpu.VMEM((3, GROUP, LEAF, RANK), F32),
+            pltpu.VMEM((2, PAR, RANK), F32),
+            pltpu.VMEM((NEAR, LEAF, LEAF), F32),
+            pltpu.VMEM((FAR, RANK, RANK), F32),
+            pltpu.VMEM((NEAR, RANK, LEAF), BF16),
+            pltpu.VMEM((NEAR, RANK, LEAF), BF16),
+            pltpu.VMEM((RANK, PAR), BF16),
+            pltpu.VMEM((RANK, PAR), BF16),
+            pltpu.SemaphoreType.DMA((4,)),
+            pltpu.SemaphoreType.DMA((COPIES,)),
+            pltpu.SemaphoreType.DMA((COPIES,)),
+        ],
+        compiler_params=pltpu.CompilerParams(collective_id=0, has_side_effects=True),
+        name="exchange",
+    )(kind, near_at, far_at, own_basis, near_blocks[0], far_coupling[0], leaf_schur, parent_basis)
 
     factor_rows, coupling_rows = pl.pallas_call(
         parent_kernel,
@@ -307,7 +388,7 @@
             pltpu.VMEM((PAR + RANK, PRED), BF16),
         ],
         name="parent",
-    )(member[None], own_rows, all_v)
+    )(member[None], all_rows, all_v)
     return (leaf_out, factor_rows, coupling_rows)
 
 

time: 573 us -> 145 us (0.25)
  the two profiles are of different devices: /device:TPU:88 before, /device:TPU:1 now
where the time goes in v2:
time: 145 us
  Pallas kernels  142 us (98%)
  other arithmetic  2.58 us (2%)
    pallas_call x1, Pallas kernels, on_device(): pl.pallas_call(exchange_kernel, out_shape=(shape(PAR, PAR), shape(PAR, PA...  91.6 us
    pallas_call x1, Pallas kernels, on_device(): pl.pallas_call(parent_kernel, out_shape=(shape(RANK, PRED), shape(RANK, P...  39.2 us
    pallas_call x1, Pallas kernels, on_device(): pl.pallas_call(leaf_kernel, out_shape=(shape(REDUN, LEAF), shape(RANK, RA...  10.9 us

profile of v2, /device:TPU:1, one launch (start us, length us, event | category | flops | bytes accessed | tf_op | source)
XLA Modules:
  0.0 144.9 jit_solution(3984267469755371572)
XLA Ops:
  0.7 0.7 and_select_fusion.1
  1.3 0.7 and_select_fusion
  2.0 0.7 select_reduce_fusion.far_at_ref
  2.6 0.6 select_reduce_fusion.1
  3.2 10.9 %leaf.1 = (f32[256,512]{1,0:T(8,128)}, f32[256,256]{1,0:T(8,128)}) custom-call(f32[512,512]{1,0:T(8,128)} %bitcast.13, f32[512,512]{1,0:T(8,128)} %bitcast.11), custom_call_target="tpu_custom_call" | custom-call | flops 2000000000 | bytes 3145728 | tf_op jit(solution)/shard_map/leaf/pallas_call | solution.py:336
  14.2 91.6 %exchange.1 = (f32[1024,1024]{1,0:T(8,128)}, f32[1024,1536]{1,0:T(8,128)}) custom-call(s32[12]{0:T(128)} %get-tuple-element.16.kind_ref, s32[12]{0:T(128)} %get-tuple-element.15.near_at_ref, s32[12]{0:T(128)} %select_reduce_fusion.far_at_ref, f32[512,512]{1,0:T(8,128)} %bitcast.12, f32[6,512,512]{2,1,0:T(8,128)} %bitcast.9, f32[5,256,256]{2,1,0:T(8,128)} %bitcast.10, ...), custom_call_target="tpu_custom_call" | custom-call | tf_op jit(solution)/shard_map/exchange/pallas_call | solution.py:353
  105.8 39.2 %parent.1 = (f32[256,768]{1,0:T(8,128)}, f32[256,768]{1,0:T(8,128)}) custom-call(s32[1]{0:T(128)} %bitcast.2.member_ref, f32[1024,1024]{1,0:T(8,128)} %get-tuple-element.11.rows_ref, f32[1024,1536]{1,0:T(8,128)} %get-tuple-element.12.v_ref), custom_call_target="tpu_custom_call" | custom-call | tf_op jit(solution)/shard_map/parent/pallas_call | solution.py:375
